TPU v7x, 32 devices: a whole 2x2x4 slice. The times are simulated.
32 devices in a mesh: level: 2 (over x), tile: 16 (over z, y, core).
Axes of the slice: x: 2, y: 2, z: 4, core: 2. Of those that a mesh axis runs over, the one named last changes fastest.
Arguments:
- density: float32 [2, 8, 8, 8, 2048], P('level', None, None, None, 'tile'), may hold values from 1 to 2
- momentum: float32 [2, 3, 8, 8, 8, 2048], P('level', None, None, None, None, 'tile'), may hold values from -0.3 to 0.3
- energy: float32 [2, 8, 8, 8, 2048], P('level', None, None, None, 'tile'), may hold values from 2.5 to 3.5
- rhs_older: float32 [2, 5, 8, 8, 8, 2048], P('level', None, None, None, None, 'tile'), may hold values from -4.5 to 4.5
- rhs_old: float32 [2, 5, 8, 8, 8, 2048], P('level', None, None, None, None, 'tile'), may hold values from -4.5 to 4.5
- peer_tile: int32 [16, 120], P('tile'), may hold values from 0 to 15, as said below
- peer_index: int32 [16, 120], P('tile'), may hold values from 0 to 119, as said below
- boundary_slot: int32 [16, 120], P('tile'), may hold values from 0 to 767, as said below
- face_partner: int32 [16, 768], P('tile'), may hold values from 0 to 767, as said below
- face_orient: int32 [16, 768], P('tile'), may hold values from 0 to 3, as said below
Outputs:
- tendency: float32 [2, 5, 8, 8, 8, 2048], P('level', None, None, None, None, 'tile')
Inputs may be any that keep to these rules, and one draw needn't show every extreme that they name: `peer_tile`: never the tile itself; the partner's partner is the face itself; every two distinct tiles share exactly 8 face pairs. `peer_index`: consistent with peer_tile: the partner face's own entries point back to this face. `boundary_slot`: distinct within a tile, and these slots are exactly the slots that face_partner maps to themselves. `face_partner`: symmetric within a tile: slots not on the boundary come in pairs that name each other; boundary slots name themselves. `face_orient`: equal at both faces of every pair, within a tile and across tiles.
All inputs are finite; a program needn't handle non-finite values.
Results may differ from a plain program's by a relative error of at most 0.0001.
Values sent between devices are 32-bit elements; how exact they have to be, the bound alone decides.
A program may use at most 384 MiB of HBM per device.

v0:
```python
import jax
import jax.numpy as jnp
import numpy as np
from jax import lax
from jax.sharding import PartitionSpec as P

NP = 8
TSTEPS = 3
FCAP = 8


step_size = 0.02
penalty = 2.5
metric = 0.1
lift_factor = 2.8
weight_back = -1.0 / 12.0
weight_here = 8.0 / 12.0
weight_next = 5.0 / 12.0


def shifted(block, axis, distance):
    devices = range(lax.axis_size(axis))
    route = [(i - distance, i) for i in devices if i - distance in devices]
    return lax.ppermute(block, axis, route)


def lobatto_points():
    degree = NP - 1
    points = np.cos(np.pi * np.arange(degree + 1) / degree)
    table = np.zeros((degree + 1, degree + 1))
    for sweep in range(60):
        table[:, 0] = 1.0
        table[:, 1] = points
        for order in range(2, degree + 1):
            table[:, order] = (
                (2 * order - 1) * points * table[:, order - 1] - (order - 1) * table[:, order - 2]
            ) / order
        points = points - (points * table[:, degree] - table[:, degree - 1]) / (
            (degree + 1) * table[:, degree]
        )
    table[:, 0] = 1.0
    table[:, 1] = points
    for order in range(2, degree + 1):
        table[:, order] = (
            (2 * order - 1) * points * table[:, order - 1] - (order - 1) * table[:, order - 2]
        ) / order
    return (points[::-1], table[::-1, degree])


def derivative_numbers():
    degree = NP - 1
    points, values = lobatto_points()
    identity = np.eye(NP)
    spread = points[:, None] - points[None, :] + identity
    table = values[:, None] / values[None, :] / spread
    table = table * (1.0 - identity)
    table[0, 0] = -degree * (degree + 1) / 4.0
    table[degree, degree] = degree * (degree + 1) / 4.0
    return np.asarray(table, dtype=np.float32)


def directional_flux(state, direction):
    density_part = state[0]
    momenta = state[1:4]
    energy_part = state[4]
    velocity = momenta / density_part
    pressure = 0.4 * (
        energy_part
        - 0.5 * (momenta[0] * velocity[0] + momenta[1] * velocity[1] + momenta[2] * velocity[2])
    )
    carried = momenta[direction]
    pieces = [carried]
    for column in range(3):
        product = carried * velocity[column]
        if column == direction:
            product = product + pressure
        pieces.append(product)
    pieces.append((energy_part + pressure) * velocity[direction])
    return jnp.stack(pieces)


def face_traces(state, tiles):
    planes = []
    for which in range(6):
        direction = which // 2
        plane = jnp.take(state, (NP - 1) * (which % 2), axis=2 + direction)
        planes.append(plane.reshape(plane.shape[:4] + (tiles, plane.shape[4] // tiles)))
    stacked = jnp.stack(planes, axis=5)
    return stacked.reshape(stacked.shape[:4] + (-1,))


def oriented(raw, orient):
    turned = raw[:, :, ::-1, ::-1, :]
    first = jnp.where(orient >= 2, turned, raw)
    second = jnp.swapaxes(first, 2, 3)
    return jnp.where(orient % 2 == 1, second, first)


def derive(field, axis, numbers):
    count = field.shape[axis]
    pieces = [lax.index_in_dim(field, index, axis, keepdims=False) for index in range(count)]
    outputs = []
    for target in range(count):
        total = None
        for index in range(count):
            factor = float(numbers[target, index])
            if factor == 0.0:
                continue
            term = factor * pieces[index]
            total = term if total is None else total + term
        outputs.append(total)
    return jnp.stack(outputs, axis=axis)


def flux_part(momenta, velocity, pressure, energy_part, direction, variable):
    carried = momenta[direction]
    if variable == 0:
        return carried
    if variable == 4:
        return (energy_part + pressure) * velocity[direction]
    product = carried * velocity[variable - 1]
    if variable - 1 == direction:
        product = product + pressure
    return product


def tendency_of(state, partner_view):
    numbers = derivative_numbers()
    density_part = state[0]
    momenta = [state[1], state[2], state[3]]
    energy_part = state[4]
    velocity = [momenta[column] / density_part for column in range(3)]
    pressure = 0.4 * (
        energy_part
        - 0.5 * (momenta[0] * velocity[0] + momenta[1] * velocity[1] + momenta[2] * velocity[2])
    )
    volumes = []
    for variable in range(5):
        total = None
        for direction in range(3):
            term = derive(
                flux_part(momenta, velocity, pressure, energy_part, direction, variable),
                -4 + direction,
                numbers,
            )
            total = term if total is None else total + term
        volumes.append(total)
    result = -metric * jnp.stack(volumes)
    traces = face_traces(state, 1)
    view = partner_view(traces)
    grouped = traces.shape[:4] + (1, 6, -1)
    own_all = traces.reshape(grouped)
    far_all = view.reshape(grouped)
    for which in range(6):
        direction = which // 2
        normal = 2.0 * (which % 2) - 1.0
        own = own_all[:, :, :, :, 0, which]
        far = far_all[:, :, :, :, 0, which]
        jump = 0.5 * normal * (
            directional_flux(far, direction) - directional_flux(own, direction)
        ) - 0.5 * penalty * (far - own)
        plane = jnp.expand_dims(-lift_factor * jump, axis=-4 + direction)
        widths = [(0, 0)] * plane.ndim
        widths[plane.ndim - 4 + direction] = (0, NP - 1) if which % 2 == 0 else (NP - 1, 0)
        result = result + jnp.pad(plane, widths)
    return result


def body(
    density,
    momentum,
    energy,
    rhs_older,
    rhs_old,
    peer_tile,
    peer_index,
    boundary_slot,
    face_partner,
    face_orient,
):
    start = jnp.concatenate([density[:, None], momentum, energy[:, None]], axis=1)[0]
    level = lax.axis_index("level")
    tiles = lax.axis_size("tile")
    peers = peer_tile[0]
    matches = peer_index[0]
    slots = boundary_slot[0]
    partner = face_partner[0]
    orient = face_orient[0]
    count = peers.shape[0]
    same_peer = peers[:, None] == peers[None, :]
    send_rank = jnp.sum(
        (same_peer & (matches[None, :] < matches[:, None])).astype(jnp.int32), axis=1
    )
    listing = jnp.arange(count, dtype=jnp.int32)
    recv_rank = jnp.sum(
        (same_peer & (listing[None, :] < listing[:, None])).astype(jnp.int32), axis=1
    )
    send_place = peers * FCAP + send_rank
    recv_place = peers * FCAP + recv_rank

    def partner_view(traces):
        raw = traces[..., partner]
        outgoing = traces[..., slots]
        buffer = (
            jnp.zeros(traces.shape[:4] + (tiles * FCAP,), jnp.float32)
            .at[..., send_place]
            .set(outgoing)
        )
        arrived = lax.all_to_all(buffer, "tile", split_axis=4, concat_axis=4, tiled=True)
        raw = raw.at[..., slots].set(arrived[..., recv_place])
        return oriented(raw, orient)

    state = start
    older = rhs_older[0]
    old = rhs_old[0]
    for repeat in range(TSTEPS):
        own_rate = tendency_of(state[:, None], partner_view)
        below = shifted(own_rate, "level", 1)[:, 0]
        own_rate = own_rate[:, 0]
        corrected = (
            state
            + step_size * (own_rate - old)
            + step_size * (weight_back * older + weight_here * old + weight_next * below)
        )
        predicted = state + step_size * own_rate
        state = jnp.where(level == 0, predicted, corrected)
        older = old
        old = below
    return ((state - start) / (TSTEPS * step_size))[None]


def solution(mesh):
    return jax.shard_map(
        body,
        mesh=mesh,
        in_specs=(
            P("level", None, None, None, "tile"),
            P("level", None, None, None, None, "tile"),
            P("level", None, None, None, "tile"),
            P("level", None, None, None, None, "tile"),
            P("level", None, None, None, None, "tile"),
            P("tile", None),
            P("tile", None),
            P("tile", None),
            P("tile", None),
            P("tile", None),
        ),
        out_specs=P("level", None, None, None, None, "tile"),
        check_vma=False,
    )
```

profile of v0, /device:TPU:0, one launch (start us, length us, event | category | flops | bytes accessed | tf_op | source)
XLA Modules:
  0.0 968.0 jit_solution(14812667734376317785)
XLA Ops:
  0.0 3.3 pad_maximum_fusion
  5.2 7.6 copy.3485
  12.8 7.8 gather_fusion.1
  23.1 18.0 %scatter_fusion = f32[5,8,8,128]{2,1,3,0:T(8,128)} fusion(f32[5,8,8,128]{2,1,3,0:T(8,128)} %broadcast.9633.clone, s32[120]{0:T(128)S(1)} %get-tuple-element.670, f32[120,5,8,8]{3,2,1,0:T(8,128)} %gather_fusion.1), kind=kCustom, calls=%fused_computation.9 | custom fusion | bytes 461280 | tf_op jit(solution)/shard_map/scatter | solution.py:207
  41.0 3.5 copy_bitcast_fusion.49
  44.5 3.7 reshape.25969
  48.2 7.6 all-to-all-start
  125.3 15.2 %gather_fusion = f32[768,5,8,8]{3,2,1,0:T(8,128)} fusion(f32[5,8,8,768]{2,1,3,0:T(8,128)} %copy.3485, s32[1024]{0:T(1024)S(1)} %pad_clamp_fusion.2), kind=kCustom, calls=%fused_computation | custom fusion | bytes 1969152 | tf_op jit(solution)/shard_map/gather | solution.py:202
  140.5 12.0 %copy.3488 = f32[5,8,8,768]{2,1,3,0:T(8,128)} copy(f32[5,8,8,768]{2,1,0,3:T(8,128)} %bitcast.2000) | data formatting | bytes 1966080 | tf_op jit(solution)/shard_map/gather | solution.py:202
  179.2 3.0 reshape.25970
  182.2 3.4 bitcast_bitcast_fusion.2
  185.7 3.9 gather_fusion.2
  189.6 18.0 %scatter_fusion.1 = f32[5,8,8,768]{2,1,3,0:T(8,128)} fusion(f32[5,8,8,768]{2,1,3,0:T(8,128)} %copy.3488, s32[120]{0:T(128)S(1)} %fusion.360, f32[120,5,8,8]{3,2,1,0:T(8,128)} %gather_fusion.2), kind=kCustom, calls=%fused_computation.10 | custom fusion | bytes 461280 | tf_op jit(solution)/shard_map/scatter | solution.py:210
  207.6 24.2 %reverse = f32[5,8,8,768]{2,1,3,0:T(8,128)} reverse(f32[5,8,8,768]{2,1,3,0:T(8,128)} %scatter_fusion.1), dimensions={1,2} | reverse | bytes 1966080
  231.8 16.6 %bitcast_select_fusion.4 = f32[5,1,8,8,768]{3,2,4,0,1:T(8,128)} fusion(f32[5,8,8,768]{2,1,3,0:T(8,128)} %scatter_fusion.1, f32[5,8,8,768]{2,1,3,0:T(8,128)} %reverse, pred[768]{0:T(1024)(128)(4,1)S(1)} %get-tuple-element.668), kind=kLoop, calls=%fused_computation.19 | loop fusion | flops 245760 | bytes 2949888 | tf_op jit(solution)/shard_map/jit(_where)/select_n | solution.py:94
  248.5 15.6 %copy.3489 = f32[5,1,8,8,768]{2,3,4,0,1:T(8,128)} copy(f32[5,1,8,8,768]{3,2,4,0,1:T(8,128)} %bitcast_select_fusion.4) | data formatting | bytes 1966080 | tf_op jit(solution)/shard_map/jit(_where)/select_n | solution.py:94
  264.1 16.6 %bitcast_select_fusion.3 = f32[5,1,8,8,768]{3,2,4,0,1:T(8,128)} fusion(f32[5,1,8,8,768]{3,2,4,0,1:T(8,128)} %bitcast_select_fusion.4, f32[5,1,8,8,768]{2,3,4,0,1:T(8,128)} %copy.3489, pred[768]{0:T(1024)(128)(4,1)S(1)} %get-tuple-element.667), kind=kLoop, calls=%fused_computation.18 | loop fusion | flops 245760 | bytes 2949888 | tf_op jit(solution)/shard_map/jit(_where)/select_n | solution.py:96
  280.7 8.5 copy.3490
  295.8 3.6 collective-permute-start
  301.7 26.3 %collective-permute-done = f32[5,1,8,8,8,128]{5,3,2,0,4,1:T(8,128)S(1)} collective-permute-done((f32[5,1,8,8,8,128]{5,3,2,0,4,1:T(8,128)}, f32[5,1,8,8,8,128]{5,3,2,0,4,1:T(8,128)S(1)}, u32[]{:S(2)}, u32[]{:S(2)}) %collective-permute-start) | collective-permute-done | bytes 1310752 | tf_op jit(solution)/shard_map/ppermute | solution.py:24
  328.7 3.1 copy_select_fusion.2
  383.8 8.7 copy.4139
  392.5 7.9 gather_fusion.4
  402.2 18.1 %scatter_fusion.2 = f32[5,8,8,128]{2,1,3,0:T(8,128)} fusion(f32[5,8,8,128]{2,1,3,0:T(8,128)} %broadcast.9633.clone.1, s32[120]{0:T(128)} %copy-done.275, f32[120,5,8,8]{3,2,1,0:T(8,128)} %gather_fusion.4), kind=kCustom, calls=%fused_computation.11 | custom fusion | bytes 461280 | tf_op jit(solution)/shard_map/scatter | solution.py:207
  420.2 3.5 copy_bitcast_fusion.48
  423.7 3.6 reshape.25971
  427.3 6.1 all-to-all-start.1
  472.0 15.2 %gather_fusion.3 = f32[768,5,8,8]{3,2,1,0:T(8,128)} fusion(f32[5,8,8,768]{2,1,3,0:T(8,128)} %copy.4139, s32[1024]{0:T(1024)S(1)} %pad_clamp_fusion.2), kind=kCustom, calls=%fused_computation.3 | custom fusion | bytes 1969152 | tf_op jit(solution)/shard_map/gather | solution.py:202
  487.3 12.0 %copy.4142 = f32[5,8,8,768]{2,1,3,0:T(8,128)} copy(f32[5,8,8,768]{2,1,0,3:T(8,128)} %bitcast.2001) | data formatting | bytes 1966080 | tf_op jit(solution)/shard_map/gather | solution.py:202
  507.2 3.0 reshape.25972
  510.2 3.4 bitcast_bitcast_fusion.1
  513.6 4.1 gather_fusion.5
  517.7 18.0 %scatter_fusion.3 = f32[5,8,8,768]{2,1,3,0:T(8,128)} fusion(f32[5,8,8,768]{2,1,3,0:T(8,128)} %copy.4142, s32[120]{0:T(128)S(1)} %fusion.360, f32[120,5,8,8]{3,2,1,0:T(8,128)} %gather_fusion.5), kind=kCustom, calls=%fused_computation.12 | custom fusion | bytes 461280 | tf_op jit(solution)/shard_map/scatter | solution.py:210
  535.7 24.2 %reverse.1 = f32[5,8,8,768]{2,1,3,0:T(8,128)} reverse(f32[5,8,8,768]{2,1,3,0:T(8,128)} %scatter_fusion.3), dimensions={1,2} | reverse | bytes 1966080
  559.8 16.6 %bitcast_select_fusion.2 = f32[5,1,8,8,768]{3,2,4,0,1:T(8,128)} fusion(f32[5,8,8,768]{2,1,3,0:T(8,128)} %scatter_fusion.3, f32[5,8,8,768]{2,1,3,0:T(8,128)} %reverse.1, pred[768]{0:T(1024)(128)(4,1)S(1)} %get-tuple-element.668), kind=kLoop, calls=%fused_computation.17 | loop fusion | flops 245760 | bytes 2949888 | tf_op jit(solution)/shard_map/jit(_where)/select_n | solution.py:94
  576.5 15.6 %copy.4143 = f32[5,1,8,8,768]{2,3,4,0,1:T(8,128)} copy(f32[5,1,8,8,768]{3,2,4,0,1:T(8,128)} %bitcast_select_fusion.2) | data formatting | bytes 1966080 | tf_op jit(solution)/shard_map/jit(_where)/select_n | solution.py:94
  592.1 16.6 %bitcast_select_fusion.1 = f32[5,1,8,8,768]{3,2,4,0,1:T(8,128)} fusion(f32[5,1,8,8,768]{3,2,4,0,1:T(8,128)} %bitcast_select_fusion.2, f32[5,1,8,8,768]{2,3,4,0,1:T(8,128)} %copy.4143, pred[768]{0:T(1024)(128)(4,1)S(1)} %get-tuple-element.667), kind=kLoop, calls=%fused_computation.16 | loop fusion | flops 245760 | bytes 2949888 | tf_op jit(solution)/shard_map/jit(_where)/select_n | solution.py:96
  608.8 9.4 copy.4144
  626.6 4.8 collective-permute-start.1
  633.1 26.7 %collective-permute-done.1 = f32[5,1,8,8,8,128]{5,4,3,2,1,0:T(8,128)S(1)} collective-permute-done((f32[5,1,8,8,8,128]{5,4,3,2,1,0:T(8,128)S(1)}, f32[5,1,8,8,8,128]{5,4,3,2,1,0:T(8,128)S(1)}, u32[]{:S(2)}, u32[]{:S(2)}) %collective-permute-start.1) | collective-permute-done | bytes 1310752 | tf_op jit(solution)/shard_map/ppermute | solution.py:24
  660.6 3.3 copy_select_fusion.1
  678.3 5.9 copy_select_fusion
  697.1 8.7 copy.4464
  705.8 7.9 gather_fusion.7
  715.4 18.1 %scatter_fusion.4 = f32[5,8,8,128]{2,1,3,0:T(8,128)} fusion(f32[5,8,8,128]{2,1,3,0:T(8,128)} %broadcast.9633, s32[120]{0:T(128)} %copy-done.275, f32[120,5,8,8]{3,2,1,0:T(8,128)} %gather_fusion.7), kind=kCustom, calls=%fused_computation.13 | custom fusion | bytes 461280 | tf_op jit(solution)/shard_map/scatter | solution.py:207
  733.5 3.5 copy_bitcast_fusion.47
  737.0 3.6 reshape.25973
  740.6 6.1 all-to-all-start.2
  765.2 2.6 add_add_fusion.7
  775.1 15.2 %gather_fusion.6 = f32[768,5,8,8]{3,2,1,0:T(8,128)} fusion(f32[5,8,8,768]{2,1,3,0:T(8,128)} %copy.4464, s32[1024]{0:T(1024)S(1)} %pad_clamp_fusion.2), kind=kCustom, calls=%fused_computation.6 | custom fusion | bytes 1969152 | tf_op jit(solution)/shard_map/gather | solution.py:202
  790.3 12.0 %copy.4467 = f32[5,8,8,768]{2,1,3,0:T(8,128)} copy(f32[5,8,8,768]{2,1,0,3:T(8,128)} %bitcast.1999) | data formatting | bytes 1966080 | tf_op jit(solution)/shard_map/gather | solution.py:202
  807.3 3.0 reshape.25974
  810.3 3.4 bitcast_bitcast_fusion
  813.7 4.1 gather_fusion.8
  817.8 18.2 %scatter_fusion.5 = f32[5,8,8,768]{2,1,3,0:T(8,128)} fusion(f32[5,8,8,768]{2,1,3,0:T(8,128)} %copy.4467, s32[120]{0:T(128)S(1)} %fusion.360, f32[120,5,8,8]{3,2,1,0:T(8,128)} %gather_fusion.8), kind=kCustom, calls=%fused_computation.14 | custom fusion | bytes 461280 | tf_op jit(solution)/shard_map/scatter | solution.py:210
  836.0 24.2 %reverse.2 = f32[5,8,8,768]{2,1,3,0:T(8,128)} reverse(f32[5,8,8,768]{2,1,3,0:T(8,128)} %scatter_fusion.5), dimensions={1,2} | reverse | bytes 1966080
  860.1 16.7 %fusion = f32[5,1,8,8,768]{2,3,4,0,1:T(8,128)} fusion(f32[5,8,8,768]{2,1,3,0:T(8,128)} %scatter_fusion.5, f32[5,8,8,768]{2,1,3,0:T(8,128)} %reverse.2, pred[768]{0:T(1024)(128)(4,1)S(1)} %get-tuple-element.668), kind=kLoop, calls=%fused_computation.21 | loop fusion | flops 245760 | bytes 2949888 | tf_op jit(solution)/shard_map/transpose | solution.py:95
  876.8 15.6 %copy.4468 = f32[5,1,8,8,768]{3,2,4,0,1:T(8,128)} copy(f32[5,1,8,8,768]{2,3,4,0,1:T(8,128)} %fusion) | data formatting | bytes 1966080 | tf_op jit(solution)/shard_map/transpose | solution.py:95
  892.4 22.3 %broadcast_select_fusion = f32[5,1,8,8,768]{3,2,4,0,1:T(8,128)} fusion(f32[5,1,8,8,768]{3,2,4,0,1:T(8,128)} %copy.4468, pred[768]{0:T(1024)(128)(4,1)S(1)} %get-tuple-element.667, f32[5,8,8,768]{2,1,3,0:T(8,128)} %scatter_fusion.5, f32[5,8,8,768]{2,1,3,0:T(8,128)} %reverse.2, pred[768]{0:T(1024)(128)(4,1)S(1)} %get-tuple-element.668), kind=kLoop, calls=%fused_computation.20 | loop fusion | flops 491520 | bytes 3933696 | tf_op jit(solution)/shard_map/jit(_where)/select_n | solution.py:96
  914.7 9.4 copy.4469
  930.0 4.6 collective-permute-start.2
  934.7 3.5 bitcast_add_fusion.1
  938.6 24.6 %collective-permute-done.2 = f32[5,1,8,8,8,128]{5,4,3,2,1,0:T(8,128)S(1)} collective-permute-done((f32[5,1,8,8,8,128]{5,4,3,2,1,0:T(8,128)S(1)}, f32[5,1,8,8,8,128]{5,4,3,2,1,0:T(8,128)S(1)}, u32[]{:S(2)}, u32[]{:S(2)}) %collective-permute-start.2) | collective-permute-done | bytes 1310752 | tf_op jit(solution)/shard_map/ppermute | solution.py:24
  963.2 4.7 fusion.3
  (1226 shorter events, 281.0 us)
Async XLA Ops:
  3.3 286.7 %copy-start.7 = (f32[5,1,8,8,8,128]{5,4,3,2,0,1:T(8,128)}, f32[5,1,8,8,8,128]{5,4,3,2,0,1:T(8,128)S(1)}, u32[]{:S(2)}) copy-start(f32[5,1,8,8,8,128]{5,4,3,2,0,1:T(8,128)S(1)} %get-tuple-element.177) | copy-start | bytes 3932164
  5.1 15.5 %copy-start.278 = (s32[1,120]{1,0:T(1,128)S(1)}, s32[1,120]{1,0:T(1,128)}, u32[]{:S(2)}) copy-start(s32[1,120]{1,0:T(1,128)} %param.27) | copy-start | bytes 1444
  5.1 15.5 %copy-start.281 = (s32[1,120]{1,0:T(1,128)S(1)}, s32[1,120]{1,0:T(1,128)}, u32[]{:S(2)}) copy-start(s32[1,120]{1,0:T(1,128)} %param.28) | copy-start | bytes 1444
  48.2 128.6 %all-to-all-start = ((f32[16,1,2560]{2,1,0:T(1,128)}), f32[16,1,2560]{2,1,0:T(1,128)}, u32[]{:S(2)}, u32[]{:S(2)}) async-start(f32[16,1,2560]{2,1,0:T(1,128)} %reshape.25969), calls=%async_computation | async-start | bytes 327680 | tf_op jit(solution)/shard_map/all_to_all | solution.py:209
  79.9 40.3 %copy-start.37 = (f32[1,8,8,1,128]{4,3,2,1,0:T(1,128)}, f32[1,8,8,1,128]{4,3,2,1,0:T(1,128)S(1)}, u32[]{:S(2)}) copy-start(f32[1,8,8,1,128]{4,3,2,1,0:T(1,128)S(1)} %broadcast.9433) | copy-start | bytes 98308
  79.9 40.2 %copy-start.39 = (f32[1,8,8,1,128]{4,3,2,1,0:T(1,128)}, f32[1,8,8,1,128]{4,3,2,1,0:T(1,128)S(1)}, u32[]{:S(2)}) copy-start(f32[1,8,8,1,128]{4,3,2,1,0:T(1,128)S(1)} %broadcast.9435) | copy-start | bytes 98308
  80.0 40.2 %copy-start.88 = (f32[1,8,8,1,128]{4,3,2,1,0:T(1,128)}, f32[1,8,8,1,128]{4,3,2,1,0:T(1,128)S(1)}, u32[]{:S(2)}) copy-start(f32[1,8,8,1,128]{4,3,2,1,0:T(1,128)S(1)} %broadcast.9437) | copy-start | bytes 98308
  80.0 40.2 %copy-start.90 = (f32[1,8,8,1,128]{4,3,2,1,0:T(1,128)}, f32[1,8,8,1,128]{4,3,2,1,0:T(1,128)S(1)}, u32[]{:S(2)}) copy-start(f32[1,8,8,1,128]{4,3,2,1,0:T(1,128)S(1)} %broadcast.9432) | copy-start | bytes 98308
  80.1 40.2 %copy-start.94 = (f32[1,8,8,1,128]{4,3,2,1,0:T(1,128)}, f32[1,8,8,1,128]{4,3,2,1,0:T(1,128)S(1)}, u32[]{:S(2)}) copy-start(f32[1,8,8,1,128]{4,3,2,1,0:T(1,128)S(1)} %broadcast.9434) | copy-start | bytes 98308
  80.1 40.1 %copy-start.98 = (f32[1,8,8,1,128]{4,3,2,1,0:T(1,128)}, f32[1,8,8,1,128]{4,3,2,1,0:T(1,128)S(1)}, u32[]{:S(2)}) copy-start(f32[1,8,8,1,128]{4,3,2,1,0:T(1,128)S(1)} %broadcast.9436) | copy-start | bytes 98308
  82.6 37.6 %copy-start.84 = (f32[1,8,8,1,128]{4,3,2,1,0:T(1,128)}, f32[1,8,8,1,128]{4,3,2,1,0:T(1,128)S(1)}, u32[]{:S(2)}) copy-start(f32[1,8,8,1,128]{4,3,2,1,0:T(1,128)S(1)} %broadcast.9445) | copy-start | bytes 98308
  86.8 35.3 %copy-start.27 = (f32[1,8,8,1,128]{4,3,2,1,0:T(1,128)}, f32[1,8,8,1,128]{4,3,2,1,0:T(1,128)S(1)}, u32[]{:S(2)}) copy-start(f32[1,8,8,1,128]{4,3,2,1,0:T(1,128)S(1)} %broadcast.9452) | copy-start | bytes 98308
  86.8 35.3 %copy-start.72 = (f32[1,8,8,1,128]{4,3,2,1,0:T(1,128)}, f32[1,8,8,1,128]{4,3,2,1,0:T(1,128)S(1)}, u32[]{:S(2)}) copy-start(f32[1,8,8,1,128]{4,3,2,1,0:T(1,128)S(1)} %broadcast.9447) | copy-start | bytes 98308
  86.8 35.2 %copy-start.66 = (f32[1,8,8,1,128]{4,3,2,1,0:T(1,128)}, f32[1,8,8,1,128]{4,3,2,1,0:T(1,128)S(1)}, u32[]{:S(2)}) copy-start(f32[1,8,8,1,128]{4,3,2,1,0:T(1,128)S(1)} %broadcast.9448) | copy-start | bytes 98308
  86.9 35.2 %copy-start.69 = (f32[1,8,8,1,128]{4,3,2,1,0:T(1,128)}, f32[1,8,8,1,128]{4,3,2,1,0:T(1,128)S(1)}, u32[]{:S(2)}) copy-start(f32[1,8,8,1,128]{4,3,2,1,0:T(1,128)S(1)} %broadcast.9449) | copy-start | bytes 98308
  86.9 35.2 %copy-start.116 = (f32[1,8,8,1,128]{4,3,2,1,0:T(1,128)}, f32[1,8,8,1,128]{4,3,2,1,0:T(1,128)S(1)}, u32[]{:S(2)}) copy-start(f32[1,8,8,1,128]{4,3,2,1,0:T(1,128)S(1)} %broadcast.9446) | copy-start | bytes 98308
  91.0 32.0 %copy-start.48 = (f32[1,8,8,1,128]{4,3,2,1,0:T(1,128)}, f32[1,8,8,1,128]{4,3,2,1,0:T(1,128)S(1)}, u32[]{:S(2)}) copy-start(f32[1,8,8,1,128]{4,3,2,1,0:T(1,128)S(1)} %broadcast.9454) | copy-start | bytes 98308
  91.1 31.9 %copy-start.42 = (f32[1,8,8,1,128]{4,3,2,1,0:T(1,128)}, f32[1,8,8,1,128]{4,3,2,1,0:T(1,128)S(1)}, u32[]{:S(2)}) copy-start(f32[1,8,8,1,128]{4,3,2,1,0:T(1,128)S(1)} %broadcast.9455) | copy-start | bytes 98308
  91.1 31.9 %copy-start.92 = (f32[1,8,8,1,128]{4,3,2,1,0:T(1,128)}, f32[1,8,8,1,128]{4,3,2,1,0:T(1,128)S(1)}, u32[]{:S(2)}) copy-start(f32[1,8,8,1,128]{4,3,2,1,0:T(1,128)S(1)} %broadcast.9453) | copy-start | bytes 98308
  91.1 31.9 %copy-start.96 = (f32[1,8,8,1,128]{4,3,2,1,0:T(1,128)}, f32[1,8,8,1,128]{4,3,2,1,0:T(1,128)S(1)}, u32[]{:S(2)}) copy-start(f32[1,8,8,1,128]{4,3,2,1,0:T(1,128)S(1)} %broadcast.9456) | copy-start | bytes 98308
  91.2 31.8 %copy-start.100 = (f32[1,8,8,1,128]{4,3,2,1,0:T(1,128)}, f32[1,8,8,1,128]{4,3,2,1,0:T(1,128)S(1)}, u32[]{:S(2)}) copy-start(f32[1,8,8,1,128]{4,3,2,1,0:T(1,128)S(1)} %broadcast.9457) | copy-start | bytes 98308
  91.2 31.8 %copy-start.102 = (f32[1,8,8,1,128]{4,3,2,1,0:T(1,128)}, f32[1,8,8,1,128]{4,3,2,1,0:T(1,128)S(1)}, u32[]{:S(2)}) copy-start(f32[1,8,8,1,128]{4,3,2,1,0:T(1,128)S(1)} %broadcast.9458) | copy-start | bytes 98308
  92.5 30.5 %copy-start.51 = (f32[1,8,8,1,128]{4,3,2,1,0:T(1,128)}, f32[1,8,8,1,128]{4,3,2,1,0:T(1,128)S(1)}, u32[]{:S(2)}) copy-start(f32[1,8,8,1,128]{4,3,2,1,0:T(1,128)S(1)} %broadcast.9461) | copy-start | bytes 98308
  92.6 30.5 %copy-start.54 = (f32[1,8,8,1,128]{4,3,2,1,0:T(1,128)}, f32[1,8,8,1,128]{4,3,2,1,0:T(1,128)S(1)}, u32[]{:S(2)}) copy-start(f32[1,8,8,1,128]{4,3,2,1,0:T(1,128)S(1)} %broadcast.9462) | copy-start | bytes 98308
  92.6 30.5 %copy-start.45 = (f32[1,8,8,1,128]{4,3,2,1,0:T(1,128)}, f32[1,8,8,1,128]{4,3,2,1,0:T(1,128)S(1)}, u32[]{:S(2)}) copy-start(f32[1,8,8,1,128]{4,3,2,1,0:T(1,128)S(1)} %broadcast.9464) | copy-start | bytes 98308
  92.6 30.9 %copy-start.104 = (f32[1,8,8,1,128]{4,3,2,1,0:T(1,128)}, f32[1,8,8,1,128]{4,3,2,1,0:T(1,128)S(1)}, u32[]{:S(2)}) copy-start(f32[1,8,8,1,128]{4,3,2,1,0:T(1,128)S(1)} %broadcast.9460) | copy-start | bytes 98308
  92.7 30.9 %copy-start.106 = (f32[1,8,8,1,128]{4,3,2,1,0:T(1,128)}, f32[1,8,8,1,128]{4,3,2,1,0:T(1,128)S(1)}, u32[]{:S(2)}) copy-start(f32[1,8,8,1,128]{4,3,2,1,0:T(1,128)S(1)} %broadcast.9463) | copy-start | bytes 98308
  92.7 30.9 %copy-start.108 = (f32[1,8,8,1,128]{4,3,2,1,0:T(1,128)}, f32[1,8,8,1,128]{4,3,2,1,0:T(1,128)S(1)}, u32[]{:S(2)}) copy-start(f32[1,8,8,1,128]{4,3,2,1,0:T(1,128)S(1)} %broadcast.9465) | copy-start | bytes 98308
  94.0 29.6 %copy-start.25 = (f32[1,8,8,1,128]{4,3,2,1,0:T(1,128)}, f32[1,8,8,1,128]{4,3,2,1,0:T(1,128)S(1)}, u32[]{:S(2)}) copy-start(f32[1,8,8,1,128]{4,3,2,1,0:T(1,128)S(1)} %broadcast.9473) | copy-start | bytes 98308
  94.0 29.6 %copy-start.60 = (f32[1,8,8,1,128]{4,3,2,1,0:T(1,128)}, f32[1,8,8,1,128]{4,3,2,1,0:T(1,128)S(1)}, u32[]{:S(2)}) copy-start(f32[1,8,8,1,128]{4,3,2,1,0:T(1,128)S(1)} %broadcast.9468) | copy-start | bytes 98308
  94.1 29.6 %copy-start.63 = (f32[1,8,8,1,128]{4,3,2,1,0:T(1,128)}, f32[1,8,8,1,128]{4,3,2,1,0:T(1,128)S(1)}, u32[]{:S(2)}) copy-start(f32[1,8,8,1,128]{4,3,2,1,0:T(1,128)S(1)} %broadcast.9469) | copy-start | bytes 98308
  94.1 29.5 %copy-start.57 = (f32[1,8,8,1,128]{4,3,2,1,0:T(1,128)}, f32[1,8,8,1,128]{4,3,2,1,0:T(1,128)S(1)}, u32[]{:S(2)}) copy-start(f32[1,8,8,1,128]{4,3,2,1,0:T(1,128)S(1)} %broadcast.9471) | copy-start | bytes 98308
  94.1 29.5 %copy-start.110 = (f32[1,8,8,1,128]{4,3,2,1,0:T(1,128)}, f32[1,8,8,1,128]{4,3,2,1,0:T(1,128)S(1)}, u32[]{:S(2)}) copy-start(f32[1,8,8,1,128]{4,3,2,1,0:T(1,128)S(1)} %broadcast.9467) | copy-start | bytes 98308
  94.2 29.5 %copy-start.112 = (f32[1,8,8,1,128]{4,3,2,1,0:T(1,128)}, f32[1,8,8,1,128]{4,3,2,1,0:T(1,128)S(1)}, u32[]{:S(2)}) copy-start(f32[1,8,8,1,128]{4,3,2,1,0:T(1,128)S(1)} %broadcast.9470) | copy-start | bytes 98308
  94.2 29.5 %copy-start.114 = (f32[1,8,8,1,128]{4,3,2,1,0:T(1,128)}, f32[1,8,8,1,128]{4,3,2,1,0:T(1,128)S(1)}, u32[]{:S(2)}) copy-start(f32[1,8,8,1,128]{4,3,2,1,0:T(1,128)S(1)} %broadcast.9472) | copy-start | bytes 98308
  95.5 28.2 %copy-start.35 = (f32[1,8,8,1,128]{4,3,2,1,0:T(1,128)}, f32[1,8,8,1,128]{4,3,2,1,0:T(1,128)S(1)}, u32[]{:S(2)}) copy-start(f32[1,8,8,1,128]{4,3,2,1,0:T(1,128)S(1)} %broadcast.9475) | copy-start | bytes 98308
  95.6 28.2 %copy-start.33 = (f32[1,8,8,1,128]{4,3,2,1,0:T(1,128)}, f32[1,8,8,1,128]{4,3,2,1,0:T(1,128)S(1)}, u32[]{:S(2)}) copy-start(f32[1,8,8,1,128]{4,3,2,1,0:T(1,128)S(1)} %broadcast.9476) | copy-start | bytes 98308
  95.6 28.1 %copy-start.31 = (f32[1,8,8,1,128]{4,3,2,1,0:T(1,128)}, f32[1,8,8,1,128]{4,3,2,1,0:T(1,128)S(1)}, u32[]{:S(2)}) copy-start(f32[1,8,8,1,128]{4,3,2,1,0:T(1,128)S(1)} %broadcast.9478) | copy-start | bytes 98308
  95.7 28.1 %copy-start.76 = (f32[1,8,8,1,128]{4,3,2,1,0:T(1,128)}, f32[1,8,8,1,128]{4,3,2,1,0:T(1,128)S(1)}, u32[]{:S(2)}) copy-start(f32[1,8,8,1,128]{4,3,2,1,0:T(1,128)S(1)} %broadcast.9474) | copy-start | bytes 98308
  95.7 28.1 %copy-start.78 = (f32[1,8,8,1,128]{4,3,2,1,0:T(1,128)}, f32[1,8,8,1,128]{4,3,2,1,0:T(1,128)S(1)}, u32[]{:S(2)}) copy-start(f32[1,8,8,1,128]{4,3,2,1,0:T(1,128)S(1)} %broadcast.9477) | copy-start | bytes 98308
  95.7 28.0 %copy-start.80 = (f32[1,8,8,1,128]{4,3,2,1,0:T(1,128)}, f32[1,8,8,1,128]{4,3,2,1,0:T(1,128)S(1)}, u32[]{:S(2)}) copy-start(f32[1,8,8,1,128]{4,3,2,1,0:T(1,128)S(1)} %broadcast.9479) | copy-start | bytes 98308
  95.8 28.0 %copy-start.82 = (f32[1,8,8,1,128]{4,3,2,1,0:T(1,128)}, f32[1,8,8,1,128]{4,3,2,1,0:T(1,128)S(1)}, u32[]{:S(2)}) copy-start(f32[1,8,8,1,128]{4,3,2,1,0:T(1,128)S(1)} %broadcast.9480) | copy-start | bytes 98308
  140.5 12.1 %copy-start.119 = (f32[5,1,8,1,8,128]{5,2,0,4,3,1:T(8,128)S(1)}, f32[5,1,8,1,8,128]{5,2,0,4,3,1:T(8,128)}, u32[]{:S(2)}) copy-start(f32[5,1,8,1,8,128]{5,2,0,4,3,1:T(8,128)} %copy-done.118) | copy-start | bytes 491524
  295.8 32.1 %collective-permute-start = (f32[5,1,8,8,8,128]{5,3,2,0,4,1:T(8,128)}, f32[5,1,8,8,8,128]{5,3,2,0,4,1:T(8,128)S(1)}, u32[]{:S(2)}, u32[]{:S(2)}) collective-permute-start(f32[5,1,8,8,8,128]{5,3,2,0,4,1:T(8,128)} %get-tuple-element.112), channel_id=1, source_target_pairs={{0,16},{1,17},{2,18},{3,19},{4,20},{5,21},{6,22},{7,23},{8,24},{9,... | collective-permute-start | bytes 3932168 | tf_op jit(solution)/shard_map/ppermute | solution.py:24
  299.5 28.5 %copy-start.15 = (f32[1,5,8,8,8,128]{5,4,3,2,1,0:T(8,128)S(1)}, f32[1,5,8,8,8,128]{5,4,3,2,1,0:T(8,128)}, u32[]{:S(2)}) copy-start(f32[1,5,8,8,8,128]{5,4,3,2,1,0:T(8,128)} %param.25) | copy-start | bytes 3932164
  301.6 27.0 %copy-start.20 = (f32[1,8,8,8,128]{4,3,2,1,0:T(8,128)S(1)}, f32[1,8,8,8,128]{4,3,2,1,0:T(8,128)}, u32[]{:S(2)}) copy-start(f32[1,8,8,8,128]{4,3,2,1,0:T(8,128)} %param.24) | copy-start | bytes 786436
  301.6 27.0 %copy-start.23 = (f32[1,8,8,8,128]{4,3,2,1,0:T(8,128)S(1)}, f32[1,8,8,8,128]{4,3,2,1,0:T(8,128)}, u32[]{:S(2)}) copy-start(f32[1,8,8,8,128]{4,3,2,1,0:T(8,128)} %param.22) | copy-start | bytes 786436
  301.6 27.0 %copy-start.30 = (f32[5,8,8,8,128]{4,2,1,0,3:T(8,128)S(1)}, f32[5,8,8,8,128]{4,2,1,0,3:T(8,128)}, u32[]{:S(2)}) copy-start(f32[5,8,8,8,128]{4,2,1,0,3:T(8,128)} %get-tuple-element.111) | copy-start | bytes 3932164
  331.8 23.0 %copy-start.1 = (f32[5,8,8,8,128]{4,3,2,1,0:T(8,128)}, f32[5,8,8,8,128]{4,3,2,1,0:T(8,128)S(1)}, u32[]{:S(2)}) copy-start(f32[5,8,8,8,128]{4,3,2,1,0:T(8,128)S(1)} %copy_select_fusion.2) | copy-start | bytes 3932164
  427.3 77.9 %all-to-all-start.1 = ((f32[16,1,2560]{2,1,0:T(1,128)}), f32[16,1,2560]{2,1,0:T(1,128)}, u32[]{:S(2)}, u32[]{:S(2)}) async-start(f32[16,1,2560]{2,1,0:T(1,128)} %reshape.25971), calls=%async_computation.1 | async-start | bytes 327680 | tf_op jit(solution)/shard_map/all_to_all | solution.py:209
  487.2 12.1 %copy-start.237 = (f32[1,8,1,8,128]{4,2,1,3,0:T(1,128)S(1)}, f32[1,8,1,8,128]{4,2,1,3,0:T(1,128)}, u32[]{:S(2)}) copy-start(f32[1,8,1,8,128]{4,2,1,3,0:T(1,128)} %get-tuple-element.502) | copy-start | bytes 98308
  487.2 12.1 %copy-start.238 = (f32[1,8,1,8,128]{4,2,1,3,0:T(1,128)S(1)}, f32[1,8,1,8,128]{4,2,1,3,0:T(1,128)}, u32[]{:S(2)}) copy-start(f32[1,8,1,8,128]{4,2,1,3,0:T(1,128)} %get-tuple-element.503) | copy-start | bytes 98308
  487.3 12.1 %copy-start.239 = (f32[1,8,1,8,128]{4,2,1,3,0:T(1,128)S(1)}, f32[1,8,1,8,128]{4,2,1,3,0:T(1,128)}, u32[]{:S(2)}) copy-start(f32[1,8,1,8,128]{4,2,1,3,0:T(1,128)} %get-tuple-element.504) | copy-start | bytes 98308
  487.3 12.1 %copy-start.240 = (f32[1,8,1,8,128]{4,2,1,3,0:T(1,128)S(1)}, f32[1,8,1,8,128]{4,2,1,3,0:T(1,128)}, u32[]{:S(2)}) copy-start(f32[1,8,1,8,128]{4,2,1,3,0:T(1,128)} %get-tuple-element.505) | copy-start | bytes 98308
  487.3 12.1 %copy-start.241 = (f32[1,8,1,8,128]{4,2,1,3,0:T(1,128)S(1)}, f32[1,8,1,8,128]{4,2,1,3,0:T(1,128)}, u32[]{:S(2)}) copy-start(f32[1,8,1,8,128]{4,2,1,3,0:T(1,128)} %get-tuple-element.506) | copy-start | bytes 98308
  487.3 12.1 %copy-start.242 = (f32[1,8,1,8,128]{4,2,1,3,0:T(1,128)S(1)}, f32[1,8,1,8,128]{4,2,1,3,0:T(1,128)}, u32[]{:S(2)}) copy-start(f32[1,8,1,8,128]{4,2,1,3,0:T(1,128)} %get-tuple-element.507) | copy-start | bytes 98308
  626.6 33.2 %collective-permute-start.1 = (f32[5,1,8,8,8,128]{5,4,3,2,1,0:T(8,128)S(1)}, f32[5,1,8,8,8,128]{5,4,3,2,1,0:T(8,128)S(1)}, u32[]{:S(2)}, u32[]{:S(2)}) collective-permute-start(f32[5,1,8,8,8,128]{5,4,3,2,1,0:T(8,128)S(1)} %pad_add_fusion.6), channel_id=1, source_target_pairs={{0,16},{1,17},{2,18},{3,19},{4,20},{5,21},{6,22},{7,23},{8,24},{9,... | collective-permute-start | bytes 3932168 | tf_op jit(solution)/shard_map/ppermute | solution.py:24
  659.8 18.3 %copy-start.3 = (f32[5,1,8,8,8,128]{5,4,3,2,1,0:T(8,128)}, f32[5,1,8,8,8,128]{5,4,3,2,1,0:T(8,128)S(1)}, u32[]{:S(2)}) copy-start(f32[5,1,8,8,8,128]{5,4,3,2,1,0:T(8,128)S(1)} %collective-permute-done.1) | copy-start | bytes 3932164
  740.6 64.7 %all-to-all-start.2 = ((f32[16,1,2560]{2,1,0:T(1,128)}), f32[16,1,2560]{2,1,0:T(1,128)}, u32[]{:S(2)}, u32[]{:S(2)}) async-start(f32[16,1,2560]{2,1,0:T(1,128)} %reshape.25973), calls=%async_computation.2 | async-start | bytes 327680 | tf_op jit(solution)/shard_map/all_to_all | solution.py:209
  790.3 13.2 %copy-start.167 = (f32[1,8,8,8,128]{4,2,1,3,0:T(8,128)S(1)}, f32[1,8,8,8,128]{4,2,1,3,0:T(8,128)}, u32[]{:S(2)}) copy-start(f32[1,8,8,8,128]{4,2,1,3,0:T(8,128)} %copy-done.166) | copy-start | bytes 786436
  930.0 33.1 %collective-permute-start.2 = (f32[5,1,8,8,8,128]{5,4,3,2,1,0:T(8,128)S(1)}, f32[5,1,8,8,8,128]{5,4,3,2,1,0:T(8,128)S(1)}, u32[]{:S(2)}, u32[]{:S(2)}) collective-permute-start(f32[5,1,8,8,8,128]{5,4,3,2,1,0:T(8,128)S(1)} %pad_add_fusion), channel_id=1, source_target_pairs={{0,16},{1,17},{2,18},{3,19},{4,20},{5,21},{6,22},{7,23},{8,24},{9,... | collective-permute-start | bytes 3932168 | tf_op jit(solution)/shard_map/ppermute | solution.py:24
  938.2 25.0 %copy-start.14 = (f32[1,3,8,8,8,128]{5,4,3,2,1,0:T(8,128)S(1)}, f32[1,3,8,8,8,128]{5,4,3,2,1,0:T(8,128)}, u32[]{:S(2)}) copy-start(f32[1,3,8,8,8,128]{5,4,3,2,1,0:T(8,128)} %param.23) | copy-start | bytes 2359300
  938.2 25.0 %copy-start.21 = (f32[1,8,8,8,128]{4,3,2,1,0:T(8,128)S(1)}, f32[1,8,8,8,128]{4,3,2,1,0:T(8,128)}, u32[]{:S(2)}) copy-start(f32[1,8,8,8,128]{4,3,2,1,0:T(8,128)} %param.24) | copy-start | bytes 786436
  938.2 25.0 %copy-start.24 = (f32[1,8,8,8,128]{4,3,2,1,0:T(8,128)S(1)}, f32[1,8,8,8,128]{4,3,2,1,0:T(8,128)}, u32[]{:S(2)}) copy-start(f32[1,8,8,8,128]{4,3,2,1,0:T(8,128)} %param.22) | copy-start | bytes 786436
  (225 other events, 802.9 us)
where the time goes:
time: 982 us; the launch traced here: 968 us
  local copies, waits for them, and re-layouts  507 us (52%)
  other arithmetic  344 us (35%)
  waiting for transfers between devices  77.5 us (8%)
  starting transfers between devices  32.9 us (3%)
    unnamed x614, local copies, waits for them, and re-layouts  123 us
    unnamed x304, other arithmetic  89.6 us
    gather x6, local copies, waits for them, and re-layouts, partner_view(): raw = traces[..., partner]  81.7 us
    ppermute x3, waiting for transfers between devices, shifted(): return lax.ppermute(block, axis, route)  77.5 us
    add x56, other arithmetic, derive(): total = term if total is None else total + term  59.4 us
    select_n x3, other arithmetic, oriented(): return jnp.where(orient % 2 == 1, second, first)  55.6 us
    scatter x3, local copies, waits for them, and re-layouts, partner_view(): raw = raw.at[..., slots].set(arrived[..., recv_place])  54.2 us
    scatter x3, local copies, waits for them, and re-layouts, partner_view(): buffer = jnp.zeros(traces.shape[:4] + (tiles * FCAP,), jnp.float32).at[.....  54.2 us
  transfers between devices with their start and end apart: 6, of which 3 were waited for; matrix products, arithmetic and copies ran while one was open for 26% of the time, Pallas kernels for 0%

commit v1 on v0

v1 whole, which is shorter than its diff:
```python
import jax
import jax.numpy as jnp
import numpy as np
from jax import lax
from jax.experimental import pallas as pl
from jax.experimental.pallas import tpu as pltpu
from jax.sharding import PartitionSpec as P

NP = 8
TSTEPS = 3
FCAP = 8


step_size = 0.02
penalty = 2.5
metric = 0.1
lift_factor = 2.8
weight_back = -1.0 / 12.0
weight_here = 8.0 / 12.0
weight_next = 5.0 / 12.0


def shifted(block, axis, distance):
    devices = range(lax.axis_size(axis))
    route = [(i - distance, i) for i in devices if i - distance in devices]
    return lax.ppermute(block, axis, route)


def lobatto_points():
    degree = NP - 1
    points = np.cos(np.pi * np.arange(degree + 1) / degree)
    table = np.zeros((degree + 1, degree + 1))
    for sweep in range(60):
        table[:, 0] = 1.0
        table[:, 1] = points
        for order in range(2, degree + 1):
            table[:, order] = (
                (2 * order - 1) * points * table[:, order - 1] - (order - 1) * table[:, order - 2]
            ) / order
        points = points - (points * table[:, degree] - table[:, degree - 1]) / (
            (degree + 1) * table[:, degree]
        )
    table[:, 0] = 1.0
    table[:, 1] = points
    for order in range(2, degree + 1):
        table[:, order] = (
            (2 * order - 1) * points * table[:, order - 1] - (order - 1) * table[:, order - 2]
        ) / order
    return (points[::-1], table[::-1, degree])


def derivative_numbers():
    degree = NP - 1
    points, values = lobatto_points()
    identity = np.eye(NP)
    spread = points[:, None] - points[None, :] + identity
    table = values[:, None] / values[None, :] / spread
    table = table * (1.0 - identity)
    table[0, 0] = -degree * (degree + 1) / 4.0
    table[degree, degree] = degree * (degree + 1) / 4.0
    return np.asarray(table, dtype=np.float32)

NV = 5
NODES = NP * NP
ROWS = NV * NODES


def primitive(w):
    inverse = 1.0 / w[0]
    velocity = [w[c] * inverse for c in (1, 2, 3)]
    pressure = 0.4 * (w[4] - 0.5 * (w[1] * velocity[0] + w[2] * velocity[1] + w[3] * velocity[2]))
    return velocity, pressure


def flux(w, velocity, pressure, direction):
    carried = w[1 + direction]
    parts = [carried]
    for column in range(3):
        product = carried * velocity[column]
        if column == direction:
            product = product + pressure
        parts.append(product)
    parts.append((w[4] + pressure) * velocity[direction])
    return parts


def pieces_of(x):
    high = x.astype(jnp.bfloat16)
    rest = x - high.astype(jnp.float32)
    middle = rest.astype(jnp.bfloat16)
    low = (rest - middle.astype(jnp.float32)).astype(jnp.bfloat16)
    return [high, middle, low]


def face_rows(which):
    direction, end = which // 2, (NP - 1) * (which % 2)
    return direction, end


def trace_rows(ref, which, v):
    direction, end = face_rows(which)
    base = v * NP * NODES
    if direction == 0:
        return ref[pl.ds(base + end * NODES, NODES), :]
    if direction == 1:
        return jnp.concatenate(
            [ref[pl.ds(base + i * NODES + end * NP, NP), :] for i in range(NP)], axis=0
        )
    return ref[pl.ds(base + end, NODES, stride=NP), :]


def trace_kernel(state, masks, turn, inner, send, raw, buffer, turned):
    width = state.shape[1]
    for which in range(6):
        lanes = pl.ds(which * width, width)
        mask = [jnp.broadcast_to(masks[o : o + 1, lanes], (NODES, width)) for o in range(4)]
        for v in range(NV):
            for at, piece in enumerate(pieces_of(trace_rows(state, which, v))):
                wide = piece.astype(jnp.float32)
                stacked = jnp.concatenate([(wide * m).astype(jnp.bfloat16) for m in mask], axis=0)
                out = jnp.dot(turn[...], stacked, preferred_element_type=jnp.float32)
                turned[at, pl.ds(v * NODES, NODES), lanes] = out.astype(jnp.bfloat16)
    total = None
    outgoing = None
    for at in range(3):
        block = turned[at]
        part = jnp.dot(block, inner[...], preferred_element_type=jnp.float32)
        leave = lax.dot_general(
            send[...], block, (((1,), (1,)), ((), ())), preferred_element_type=jnp.float32
        )
        total = part if total is None else total + part
        outgoing = leave if outgoing is None else outgoing + leave
    raw[...] = total
    buffer[...] = outgoing


def rate_kernel(state, raw, arrived, place, rolled, rate, view):
    width = state.shape[1]
    numbers = derivative_numbers()
    total = raw[...]
    for piece in pieces_of(arrived[...]):
        total = total + lax.dot_general(
            piece, place[...], (((0,), (0,)), ((), ())), preferred_element_type=jnp.float32
        )
    view[...] = total

    def combine(fields, target):
        result = None
        for index in range(NP):
            factor = float(-metric * numbers[target, index])
            if factor == 0.0:
                continue
            term = factor * fields[index]
            result = term if result is None else result + term
        return result

    def at(v, i, j):
        return pl.ds(pl.multiple_of(v * NP * NODES + i * NODES + j * NP, NP), NP)

    def along_first(j, carry):
        across = [[None] * NP for v in range(NV)]
        down = [[None] * NP for v in range(NV)]
        for i in range(NP):
            w = [state[at(v, i, j), :] for v in range(NV)]
            velocity, pressure = primitive(w)
            for v, part in enumerate(flux(w, velocity, pressure, 0)):
                across[v][i] = part
            for v, part in enumerate(flux(w, velocity, pressure, 2)):
                total = rolled[0] * part
                for shift in range(1, NP):
                    total = total + rolled[shift] * pltpu.roll(part, NP - shift, 0)
                down[v][i] = total
        for v in range(NV):
            for i in range(NP):
                rate[at(v, i, j), :] = combine(across[v], i) + down[v][i]
        return carry

    def along_second(i, carry):
        across = [[None] * NP for v in range(NV)]
        for j in range(NP):
            w = [state[at(v, i, j), :] for v in range(NV)]
            velocity, pressure = primitive(w)
            for v, part in enumerate(flux(w, velocity, pressure, 1)):
                across[v][j] = part
        for v in range(NV):
            for j in range(NP):
                rate[at(v, i, j), :] = rate[at(v, i, j), :] + combine(across[v], j)
        return carry

    lax.fori_loop(0, NP, along_first, 0)
    lax.fori_loop(0, NP, along_second, 0)

    for which in range(6):
        direction, end = face_rows(which)
        normal = 2.0 * (which % 2) - 1.0
        lanes = pl.ds(which * width, width)

        def lift(row, carry):
            def rows(v):
                base = v * NP * NODES
                if direction == 0:
                    return pl.ds(pl.multiple_of(base + end * NODES + row * NP, NP), NP)
                if direction == 1:
                    return pl.ds(pl.multiple_of(base + row * NODES + end * NP, NP), NP)
                return pl.ds(base + row * NODES + end, NP, stride=NP)

            own = [state[rows(v), :] for v in range(NV)]
            far = [
                view[pl.ds(pl.multiple_of(v * NODES + row * NP, NP), NP), lanes]
                for v in range(NV)
            ]
            own_flux = flux(own, *primitive(own), direction)
            far_flux = flux(far, *primitive(far), direction)
            for v in range(NV):
                jump = (0.5 * normal) * (far_flux[v] - own_flux[v]) - (0.5 * penalty) * (
                    far[v] - own[v]
                )
                rate[rows(v), :] = rate[rows(v), :] - lift_factor * jump
            return carry

        lax.fori_loop(0, NP, lift, 0)


VMEM = pl.BlockSpec(memory_space=pltpu.VMEM)


def traces_of(state, masks, turn, inner, send):
    slots = masks.shape[1]
    return pl.pallas_call(
        trace_kernel,
        out_shape=(
            jax.ShapeDtypeStruct((ROWS, slots), jnp.float32),
            jax.ShapeDtypeStruct((send.shape[0], ROWS), jnp.float32),
        ),
        in_specs=[VMEM] * 5,
        out_specs=(VMEM, VMEM),
        scratch_shapes=[pltpu.VMEM((3, ROWS, slots), jnp.bfloat16)],
        compiler_params=pltpu.CompilerParams(vmem_limit_bytes=40 << 20),
    )(state, masks, turn, inner, send)


def rate_of(state, raw, arrived, place, rolled):
    return pl.pallas_call(
        rate_kernel,
        out_shape=jax.ShapeDtypeStruct(state.shape, jnp.float32),
        in_specs=[VMEM] * 5,
        out_specs=VMEM,
        scratch_shapes=[pltpu.VMEM(raw.shape, jnp.float32)],
        compiler_params=pltpu.CompilerParams(vmem_limit_bytes=40 << 20),
    )(state, raw, arrived, place, rolled)


def turning():
    nodes = np.arange(NODES)
    blocks = []
    for orient in range(4):
        source = nodes.reshape(NP, NP)
        if orient >= 2:
            source = source[::-1, ::-1]
        if orient % 2 == 1:
            source = source.T
        block = np.zeros((NODES, NODES), np.float32)
        block[nodes, source.reshape(-1)] = 1.0
        blocks.append(block)
    return np.concatenate(blocks, axis=1)


def body(
    density,
    momentum,
    energy,
    rhs_older,
    rhs_old,
    peer_tile,
    peer_index,
    boundary_slot,
    face_partner,
    face_orient,
):
    width = density.shape[-1]
    start = jnp.concatenate(
        [
            density.reshape(-1, width),
            momentum.reshape(-1, width),
            energy.reshape(-1, width),
        ],
        axis=0,
    )
    level = lax.axis_index("level")
    levels = lax.axis_size("level")
    tiles = lax.axis_size("tile")
    peers = peer_tile[0]
    matches = peer_index[0]
    slots = boundary_slot[0]
    partner = face_partner[0]
    orient = face_orient[0]
    count = peers.shape[0]
    faces = partner.shape[0]
    same_peer = peers[:, None] == peers[None, :]
    listing = jnp.arange(count, dtype=jnp.int32)
    send_rank = jnp.sum(same_peer & (matches[None, :] < matches[:, None]), axis=1, dtype=jnp.int32)
    recv_rank = jnp.sum(same_peer & (listing[None, :] < listing[:, None]), axis=1, dtype=jnp.int32)
    places = jnp.arange(tiles * FCAP, dtype=jnp.int32)
    ids = jnp.arange(faces, dtype=jnp.int32)
    exact = jnp.bfloat16
    at_slot = (slots[:, None] == ids[None, :]).astype(exact)

    def routing(rank):
        onehot = (places[:, None] == (peers * FCAP + rank)[None, :]).astype(exact)
        return jnp.dot(onehot, at_slot, preferred_element_type=jnp.float32).astype(exact)

    send = routing(send_rank)
    place = routing(recv_rank)
    inner = ((ids[:, None] == partner[None, :]) & (partner != ids)[None, :]).astype(exact)
    masks = (orient[None, :] == jnp.arange(8, dtype=jnp.int32)[:, None]).astype(jnp.float32)
    turn = jnp.asarray(turning(), exact)
    numbers = derivative_numbers()
    diagonals = np.stack(
        [
            np.stack([-metric * numbers[k, (k + shift) % NP] for k in range(NP)])
            for shift in range(NP)
        ]
    ).astype(np.float32)
    rolled = jnp.broadcast_to(jnp.asarray(diagonals)[:, :, None], (NP, NP, width))

    def rates(states):
        traced = [traces_of(state, masks, turn, inner, send) for state in states]
        buffer = jnp.concatenate([leave for raw, leave in traced], axis=1)
        arrived = lax.all_to_all(buffer, "tile", split_axis=0, concat_axis=0, tiled=True)
        return [
            rate_of(state, raw, arrived[:, at * ROWS : (at + 1) * ROWS], place, rolled)
            for at, (state, (raw, leave)) in enumerate(zip(states, traced))
        ]

    older = rhs_older.reshape(-1, width)
    old = rhs_old.reshape(-1, width)

    def advance(state, own_rate, older, old, below):
        corrected = (
            state
            + step_size * (own_rate - old)
            + step_size * (weight_back * older + weight_here * old + weight_next * below)
        )
        return jnp.where(level == 0, state + step_size * own_rate, corrected)

    state = start
    if levels == 2:
        received = shifted(start, "level", 1)
        own_rate = rates([state])[0]
        received, own_rate = lax.optimization_barrier((received, own_rate))
        lower = jnp.where(level == 0, start, received)
        for repeat in range(TSTEPS):
            if repeat == 0:
                below = rates([lower])[0]
            else:
                own_rate, below = rates([state, lower])
            state = advance(state, own_rate, older, old, below)
            lower = lower + step_size * below
            older = old
            old = below
    else:
        for repeat in range(TSTEPS):
            own_rate = rates([state])[0]
            below = shifted(own_rate, "level", 1)
            state = advance(state, own_rate, older, old, below)
            older = old
            old = below
    return ((state - start) / (TSTEPS * step_size)).reshape(rhs_old.shape)


def solution(mesh):
    return jax.shard_map(
        body,
        mesh=mesh,
        in_specs=(
            P("level", None, None, None, "tile"),
            P("level", None, None, None, None, "tile"),
            P("level", None, None, None, "tile"),
            P("level", None, None, None, None, "tile"),
            P("level", None, None, None, None, "tile"),
            P("tile", None),
            P("tile", None),
            P("tile", None),
            P("tile", None),
            P("tile", None),
        ),
        out_specs=P("level", None, None, None, None, "tile"),
        check_vma=False,
    )
```

time: 982 us -> 123 us (0.13); the launches traced: 968 us -> 122 us
  local copies, waits for them, and re-layouts: 507 us -> 5.71 us
  other arithmetic: 344 us -> 9.7 us
  waiting for transfers between devices: 77.5 us -> 15.1 us
  Pallas kernels: 0 us -> 44.9 us
  blocking collectives: 0 us -> 27.9 us
  starting transfers between devices: 32.9 us -> 17.4 us
    gather x18 -> x0, local copies, waits for them, and re-layouts: 122 us -> none  [the longest x6 81.7 us: partner_view(): raw = traces[..., partner]]
    unnamed x614 -> x40, local copies, waits for them, and re-layouts: 123 us -> 5.43 us
    scatter x6 -> x0, local copies, waits for them, and re-layouts: 108 us -> none  [the longest x3 54.2 us: partner_view(): raw = raw.at[..., slots].set(arrived[..., recv_place])]
    select_n x12 -> x3, other arithmetic: 104 us -> 3.01 us  [the longest x2 2.79 us: advance(): return jnp.where(level == 0, state + step_size * own_rate, corrected)]
    unnamed x304 -> x2, other arithmetic: 89.6 us -> 0.03 us
    ppermute x3 -> x1, waiting for transfers between devices: 77.5 us -> 0.01 us  [shifted(): return lax.ppermute(block, axis, route)]
    add x63 -> x0, other arithmetic: 67.8 us -> none  [the longest x56 59.4 us: derive(): total = term if total is None else total + term]
    select_n x5 -> x0, local copies, waits for them, and re-layouts: 58.6 us -> none  [the longest x2 31.3 us: oriented(): first = jnp.where(orient >= 2, turned, raw)]
  transfers between devices with their start and end apart: 6 -> 3, of which waited for: 3 -> 2; matrix products, arithmetic and copies ran while one was open for 26% -> 3% of each run, Pallas kernels for 0% -> 7%
where the time goes in v1:
time: 123 us; the launch traced here: 122 us
  Pallas kernels  44.9 us (37%)
  blocking collectives  27.9 us (23%)
  starting transfers between devices  17.4 us (14%)
  waiting for transfers between devices  15.1 us (12%)
  other arithmetic  9.7 us (8%)
  local copies, waits for them, and re-layouts  5.71 us (5%)
    all_to_all x2, blocking collectives, rates(): lax.all_to_all(buffer, 'tile', split_axis=0, concat_axis=0, tiled=True)  27.9 us
    pallas_call x6, Pallas kernels, rate_of(): pl.pallas_call(rate_kernel, out_shape=jax.ShapeDtypeStruct(state.shape, j...  26.3 us
    pallas_call x6, Pallas kernels, traces_of(): pl.pallas_call(trace_kernel, out_shape=(jax.ShapeDtypeStruct((ROWS, slots...  18.6 us
    all_to_all x2, waiting for transfers between devices, rates(): lax.all_to_all(buffer, 'tile', split_axis=0, concat_axis=0, tiled=True)  15.1 us
    all_to_all x2, starting transfers between devices, rates(): lax.all_to_all(buffer, 'tile', split_axis=0, concat_axis=0, tiled=True)  11.5 us
    ppermute x1, starting transfers between devices, shifted(): return lax.ppermute(block, axis, route)  5.91 us
    unnamed x40, local copies, waits for them, and re-layouts  5.43 us
    select_n x2, other arithmetic, advance(): return jnp.where(level == 0, state + step_size * own_rate, corrected)  2.79 us
  transfers between devices with their start and end apart: 3, of which 2 were waited for; matrix products, arithmetic and copies ran while one was open for 3% of the time, Pallas kernels for 7%

profile of v1, /device:TPU:0, one launch (start us, length us, event | category | flops | bytes accessed | tf_op | source)
XLA Modules:
  0.0 121.6 jit_solution(18331919376128021566)
XLA Ops:
  0.0 0.0 copy-start.17
  0.0 0.0 copy-start.14
  0.0 0.0 copy-start.15
  0.0 0.0 copy-start.19
  0.0 0.0 copy-start.18
  0.0 1.4 %pad_maximum_fusion.state = f32[2560,128]{1,0:T(8,128)S(1)} fusion(f32[512,128]{1,0:T(8,128)} %bitcast.67, f32[1536,128]{1,0:T(8,128)} %bitcast.63, f32[512,128]{1,0:T(8,128)} %bitcast.71), kind=kLoop, calls=%fused_computation.3 | loop fusion | flops 655360 | bytes 2621440 | tf_op jit(solution)/shard_map/concatenate | solution.py:281
  1.4 0.0 copy-start.2
  1.4 5.9 %collective-permute-start = (f32[2560,128]{1,0:T(8,128)S(1)}, f32[2560,128]{1,0:T(8,128)}, u32[]{:S(2)}, u32[]{:S(2)}) collective-permute-start(f32[2560,128]{1,0:T(8,128)S(1)} %pad_maximum_fusion.state), channel_id=1, source_target_pairs={{0,16},{1,17},{2,18},{3,19},{4,20},{5,21},{6,22},{7,23},{8,24},{9,... | collective-permute-start | bytes 3932168 | tf_op jit(solution)/shard_map/ppermute | solution.py:26
  7.4 0.0 copy-done.17
  7.4 0.0 copy-done.14
  7.4 0.0 copy-done.15
  7.4 0.0 copy-done.19
  7.4 0.2 convert_reduce_fusion
  7.7 0.0 copy-done.18
  7.7 0.3 convolution_convert_fusion.1.send
  8.0 0.5 fusion.1.inner
  8.4 0.0 copy-done.2
  8.5 0.0 copy-start.16
  8.5 3.5 %shard_map.118 = (f32[320,768]{1,0:T(8,128)S(1)}, f32[128,320]{1,0:T(8,128)}) custom-call(f32[2560,128]{1,0:T(8,128)S(1)} %pad_maximum_fusion.state, f32[8,768]{1,0:T(8,128)S(1)} %fusion.17.masks, bf16[64,256]{1,0:T(8,128)(2,1)S(1)} %copy-done.2, bf16[768,768]{1,0:T(8,128)(2,1)S(1)} %fusion.1.inner, bf16[128,768]{1,0:T(8,128)(2,1)S(1)} %convolution_convert_fusion.1.send), custom_call_target="tpu_custom_call" | custom-call | tf_op jit(solution)/shard_map/pallas_call | solution.py:229
  12.0 0.9 copy-done.3
  13.0 5.9 %all-to-all-start = ((f32[16,8,320]{2,1,0:T(8,128)}), f32[16,8,320]{2,1,0:T(8,128)S(1)}, u32[]{:S(2)}, u32[]{:S(2)}) async-start(f32[16,8,320]{2,1,0:T(8,128)} %bitcast.8), calls=%async_computation | async-start | bytes 393216 | tf_op jit(solution)/shard_map/all_to_all | solution.py:329
  18.9 0.3 convolution_convert_fusion.place
  19.2 8.7 %all-to-all-done = f32[16,8,320]{2,1,0:T(8,128)S(1)} async-done(((f32[16,8,320]{2,1,0:T(8,128)}), f32[16,8,320]{2,1,0:T(8,128)S(1)}, u32[]{:S(2)}, u32[]{:S(2)}) %all-to-all-start) | async-done | bytes 163872 | tf_op jit(solution)/shard_map/all_to_all | solution.py:329
  27.9 0.0 copy-done.16
  27.9 0.1 broadcast_in_dim.2.rolled
  28.0 1.2 copy-done.4
  29.2 4.4 %shard_map.119 = f32[2560,128]{1,0:T(8,128)S(1)} custom-call(f32[2560,128]{1,0:T(8,128)S(1)} %pad_maximum_fusion.state, f32[320,768]{1,0:T(8,128)S(1)} %copy-done.4, f32[128,320]{1,0:T(8,128)S(1)} %bitcast.61, bf16[128,768]{1,0:T(8,128)(2,1)S(1)} %convolution_convert_fusion.place, f32[8,8,128]{2,1,0:T(8,128)S(1)} %broadcast_in_dim.2.rolled), custom_call_target="tpu_custom_call" | custom-call | tf_op jit(solution)/shard_map/pallas_call | solution.py:243
  33.6 0.0 copy-start
  33.6 1.1 copy-done
  34.6 0.0 collective-permute-done
  34.6 0.0 copy-done.7
  34.6 0.0 copy-done.11
  34.6 0.0 copy-done.12
  34.7 0.2 broadcast_select_fusion.state
  34.9 3.6 %shard_map.120 = (f32[320,768]{1,0:T(8,128)S(1)}, f32[128,320]{1,0:T(8,128)}) custom-call(f32[2560,128]{1,0:T(8,128)S(1)} %broadcast_select_fusion.state, f32[8,768]{1,0:T(8,128)S(1)} %fusion.17.masks, bf16[64,256]{1,0:T(8,128)(2,1)S(1)} %copy-done.2, bf16[768,768]{1,0:T(8,128)(2,1)S(1)} %fusion.1.inner, bf16[128,768]{1,0:T(8,128)(2,1)S(1)} %convolution_convert_fusion.1.send), custom_call_target="tpu_custom_call" | custom-call | tf_op jit(solution)/shard_map/pallas_call | solution.py:229
  38.4 0.9 copy-done.5
  39.4 5.6 %all-to-all-start.1 = ((f32[16,8,320]{2,1,0:T(8,128)}), f32[16,8,320]{2,1,0:T(8,128)S(1)}, u32[]{:S(2)}, u32[]{:S(2)}) async-start(f32[16,8,320]{2,1,0:T(8,128)} %bitcast.14), calls=%async_computation.1 | async-start | bytes 393216 | tf_op jit(solution)/shard_map/all_to_all | solution.py:329
  45.0 2.6 %broadcast_multiply_fusion = f32[1,5,8,8,8,128]{5,4,3,2,1,0:T(8,128)} fusion(f32[1,5,8,8,8,128]{5,4,3,2,1,0:T(8,128)} %param.15), kind=kLoop, calls=%fused_computation.24 | loop fusion | flops 327680 | bytes 2621440 | tf_op jit(solution)/shard_map/mul | solution.py:342
  47.6 6.4 %all-to-all-done.1 = f32[16,8,320]{2,1,0:T(8,128)S(1)} async-done(((f32[16,8,320]{2,1,0:T(8,128)}), f32[16,8,320]{2,1,0:T(8,128)S(1)}, u32[]{:S(2)}, u32[]{:S(2)}) %all-to-all-start.1) | async-done | bytes 163872 | tf_op jit(solution)/shard_map/all_to_all | solution.py:329
  54.0 1.2 copy-done.6
  55.2 4.4 %shard_map.121 = f32[2560,128]{1,0:T(8,128)S(1)} custom-call(f32[2560,128]{1,0:T(8,128)S(1)} %broadcast_select_fusion.state, f32[320,768]{1,0:T(8,128)S(1)} %copy-done.6, f32[128,320]{1,0:T(8,128)S(1)} %bitcast.62, bf16[128,768]{1,0:T(8,128)(2,1)S(1)} %convolution_convert_fusion.place, f32[8,8,128]{2,1,0:T(8,128)S(1)} %broadcast_in_dim.2.rolled), custom_call_target="tpu_custom_call" | custom-call | tf_op jit(solution)/shard_map/pallas_call | solution.py:243
  59.6 0.0 copy-done.1
  59.6 0.0 copy-done.8
  59.6 0.0 copy-done.9
  59.6 0.0 copy-done.13
  59.6 2.1 %fusion.5 = (f32[2560,128]{1,0:T(8,128)S(1)}, f32[2560,128]{1,0:T(8,128)S(1)}) fusion(f32[1,5,8,8,8,128]{5,4,3,2,1,0:T(8,128)S(1)} %copy-done.9, f32[2560,128]{1,0:T(8,128)S(1)} %copy-done.1, f32[1,5,8,8,8,128]{5,4,3,2,1,0:T(8,128)} %param.16, f32[2560,128]{1,0:T(8,128)S(1)} %shard_map.121, pred[]{:T(512)S(6)} %eq.96, f32[512,128]{1,0:T(8,128)S(1)} %bitcast.69, ...), kind=kLoop, calls=%fused_computation.8 | loop fusion | flops 5242880 | bytes 10485761 | tf_op jit(solution)/shard_map/jit(_where)/select_n | solution.py:344
  61.8 2.9 %shard_map.122 = (f32[320,768]{1,0:T(8,128)S(1)}, f32[128,320]{1,0:T(8,128)S(1)}) custom-call(f32[2560,128]{1,0:T(8,128)S(1)} %get-tuple-element.37.state, f32[8,768]{1,0:T(8,128)S(1)} %fusion.17.masks, bf16[64,256]{1,0:T(8,128)(2,1)S(1)} %copy-done.2, bf16[768,768]{1,0:T(8,128)(2,1)S(1)} %fusion.1.inner, bf16[128,768]{1,0:T(8,128)(2,1)S(1)} %convolution_convert_fusion.1.send), custom_call_target="tpu_custom_call" | custom-call | tf_op jit(solution)/shard_map/pallas_call | solution.py:229
  64.6 2.9 %shard_map.123 = (f32[320,768]{1,0:T(8,128)S(1)}, f32[128,320]{1,0:T(8,128)S(1)}) custom-call(f32[2560,128]{1,0:T(8,128)S(1)} %get-tuple-element.38.state, f32[8,768]{1,0:T(8,128)S(1)} %fusion.17.masks, bf16[64,256]{1,0:T(8,128)(2,1)S(1)} %copy-done.2, bf16[768,768]{1,0:T(8,128)(2,1)S(1)} %fusion.1.inner, bf16[128,768]{1,0:T(8,128)(2,1)S(1)} %convolution_convert_fusion.1.send), custom_call_target="tpu_custom_call" | custom-call | tf_op jit(solution)/shard_map/pallas_call | solution.py:229
  67.5 0.1 maximum_bitcast_fusion
  67.6 13.7 %all_to_all.46 = f32[16,8,640]{2,1,0:T(8,128)S(1)} all-to-all(f32[16,8,640]{2,1,0:T(8,128)S(1)} %maximum_bitcast_fusion), channel_id=1, replica_groups=mesh['level'=2,'tile'=16] {'tile'}, dimensions={0} | all-to-all | bytes 655360 | tf_op jit(solution)/shard_map/all_to_all | solution.py:329
  81.3 0.1 fusion.21
  81.4 4.4 %shard_map.124 = f32[2560,128]{1,0:T(8,128)S(1)} custom-call(f32[2560,128]{1,0:T(8,128)S(1)} %get-tuple-element.37.state, f32[320,768]{1,0:T(8,128)S(1)} %get-tuple-element.25.raw, f32[128,320]{1,0:T(8,128)S(1)} %get-tuple-element.41.arrived, bf16[128,768]{1,0:T(8,128)(2,1)S(1)} %convolution_convert_fusion.place, f32[8,8,128]{2,1,0:T(8,128)S(1)} %broadcast_in_dim.2.rolled), custom_call_target="tpu_custom_call" | custom-call | tf_op jit(solution)/shard_map/pallas_call | solution.py:243
  85.8 0.0 copy-start.10
  85.8 4.4 %shard_map.125 = f32[2560,128]{1,0:T(8,128)S(1)} custom-call(f32[2560,128]{1,0:T(8,128)S(1)} %get-tuple-element.38.state, f32[320,768]{1,0:T(8,128)S(1)} %get-tuple-element.28.raw, f32[128,320]{1,0:T(8,128)S(1)} %get-tuple-element.42.arrived, bf16[128,768]{1,0:T(8,128)(2,1)S(1)} %convolution_convert_fusion.place, f32[8,8,128]{2,1,0:T(8,128)S(1)} %broadcast_in_dim.2.rolled), custom_call_target="tpu_custom_call" | custom-call | tf_op jit(solution)/shard_map/pallas_call | solution.py:243
  90.2 0.0 copy-done.10
  90.2 0.6 fusion.12
  90.9 2.9 %shard_map.127 = (f32[320,768]{1,0:T(8,128)S(1)}, f32[128,320]{1,0:T(8,128)S(1)}) custom-call(f32[2560,128]{1,0:T(8,128)S(1)} %get-tuple-element.36.state, f32[8,768]{1,0:T(8,128)S(1)} %fusion.17.masks, bf16[64,256]{1,0:T(8,128)(2,1)S(1)} %copy-done.2, bf16[768,768]{1,0:T(8,128)(2,1)S(1)} %fusion.1.inner, bf16[128,768]{1,0:T(8,128)(2,1)S(1)} %convolution_convert_fusion.1.send), custom_call_target="tpu_custom_call" | custom-call | tf_op jit(solution)/shard_map/pallas_call | solution.py:229
  93.8 2.9 %shard_map.126 = (f32[320,768]{1,0:T(8,128)S(1)}, f32[128,320]{1,0:T(8,128)S(1)}) custom-call(f32[2560,128]{1,0:T(8,128)S(1)} %get-tuple-element.35.state, f32[8,768]{1,0:T(8,128)S(1)} %fusion.17.masks, bf16[64,256]{1,0:T(8,128)(2,1)S(1)} %copy-done.2, bf16[768,768]{1,0:T(8,128)(2,1)S(1)} %fusion.1.inner, bf16[128,768]{1,0:T(8,128)(2,1)S(1)} %convolution_convert_fusion.1.send), custom_call_target="tpu_custom_call" | custom-call | tf_op jit(solution)/shard_map/pallas_call | solution.py:229
  96.6 0.1 maximum_bitcast_fusion.1
  96.7 14.2 %all_to_all.47 = f32[16,8,640]{2,1,0:T(8,128)S(1)} all-to-all(f32[16,8,640]{2,1,0:T(8,128)S(1)} %maximum_bitcast_fusion.1), channel_id=1, replica_groups=mesh['level'=2,'tile'=16] {'tile'}, dimensions={0} | all-to-all | bytes 655360 | tf_op jit(solution)/shard_map/all_to_all | solution.py:329
  111.0 0.1 fusion.20
  111.1 4.4 %shard_map.129 = f32[2560,128]{1,0:T(8,128)S(1)} custom-call(f32[2560,128]{1,0:T(8,128)S(1)} %get-tuple-element.36.state, f32[320,768]{1,0:T(8,128)S(1)} %get-tuple-element.32.raw, f32[128,320]{1,0:T(8,128)S(1)} %get-tuple-element.40.arrived, bf16[128,768]{1,0:T(8,128)(2,1)S(1)} %convolution_convert_fusion.place, f32[8,8,128]{2,1,0:T(8,128)S(1)} %broadcast_in_dim.2.rolled), custom_call_target="tpu_custom_call" | custom-call | tf_op jit(solution)/shard_map/pallas_call | solution.py:243
  115.5 4.4 %shard_map.128 = f32[2560,128]{1,0:T(8,128)S(1)} custom-call(f32[2560,128]{1,0:T(8,128)S(1)} %get-tuple-element.35.state, f32[320,768]{1,0:T(8,128)S(1)} %get-tuple-element.29.raw, f32[128,320]{1,0:T(8,128)S(1)} %get-tuple-element.39.arrived, bf16[128,768]{1,0:T(8,128)(2,1)S(1)} %convolution_convert_fusion.place, f32[8,8,128]{2,1,0:T(8,128)S(1)} %broadcast_in_dim.2.rolled), custom_call_target="tpu_custom_call" | custom-call | tf_op jit(solution)/shard_map/pallas_call | solution.py:243
  119.9 1.7 %subtract_multiply_fusion = f32[2560,128]{1,0:T(8,128)} fusion(f32[2560,128]{1,0:T(8,128)S(1)} %shard_map.129, f32[2560,128]{1,0:T(8,128)S(1)} %shard_map.125, f32[2560,128]{1,0:T(8,128)S(1)} %shard_map.121, f32[2560,128]{1,0:T(8,128)S(1)} %get-tuple-element.35.state, f32[2560,128]{1,0:T(8,128)S(1)} %shard_map.128, pred[]{:T(512)S(6)} %eq.96, ...), kind=kLoop, calls=%fused_computation.19 | loop fusion | flops 5570560 | bytes 9175041 | tf_op jit(solution)/shard_map/div | solution.py:368
  (16 shorter events, 0.1 us)
Async XLA Ops:
  0.0 7.4 %copy-start.17 = (s32[1,768]{1,0:T(1,128)S(1)}, s32[1,768]{1,0:T(1,128)}, u32[]{:S(2)}) copy-start(s32[1,768]{1,0:T(1,128)} %param.21) | copy-start | bytes 9220
  0.0 7.4 %copy-start.14 = (s32[1,768]{1,0:T(1,128)S(1)}, s32[1,768]{1,0:T(1,128)}, u32[]{:S(2)}) copy-start(s32[1,768]{1,0:T(1,128)} %param.20) | copy-start | bytes 9220
  0.0 7.4 %copy-start.15 = (s32[1,120]{1,0:T(1,128)S(1)}, s32[1,120]{1,0:T(1,128)}, u32[]{:S(2)}) copy-start(s32[1,120]{1,0:T(1,128)} %param.17) | copy-start | bytes 1444
  0.0 7.4 %copy-start.19 = (s32[1,120]{1,0:T(1,128)S(1)}, s32[1,120]{1,0:T(1,128)}, u32[]{:S(2)}) copy-start(s32[1,120]{1,0:T(1,128)} %param.18) | copy-start | bytes 1444
  0.0 7.7 %copy-start.18 = (s32[1,120]{1,0:T(1,128)S(1)}, s32[1,120]{1,0:T(1,128)}, u32[]{:S(2)}) copy-start(s32[1,120]{1,0:T(1,128)} %param.19) | copy-start | bytes 1444
  1.4 7.0 %copy-start.2 = (bf16[64,256]{1,0:T(8,128)(2,1)S(1)}, bf16[64,256]{1,0:T(8,128)(2,1)}, u32[]{:S(2)}) copy-start(bf16[64,256]{1,0:T(8,128)(2,1)} %constant.25.clone.turn) | copy-start | bytes 98308
  1.4 33.2 %collective-permute-start = (f32[2560,128]{1,0:T(8,128)S(1)}, f32[2560,128]{1,0:T(8,128)}, u32[]{:S(2)}, u32[]{:S(2)}) collective-permute-start(f32[2560,128]{1,0:T(8,128)S(1)} %pad_maximum_fusion.state), channel_id=1, source_target_pairs={{0,16},{1,17},{2,18},{3,19},{4,20},{5,21},{6,22},{7,23},{8,24},{9,... | collective-permute-start | bytes 3932168 | tf_op jit(solution)/shard_map/ppermute | solution.py:26
  8.5 19.4 %copy-start.16 = (f32[8,8]{1,0:T(8,128)S(1)}, f32[8,8]{1,0:T(8,128)}, u32[]{:S(2)}) copy-start(f32[8,8]{1,0:T(8,128)} %constant.26.clone) | copy-start | bytes 772
  12.0 0.9 copy-start.3
  13.0 14.9 %all-to-all-start = ((f32[16,8,320]{2,1,0:T(8,128)}), f32[16,8,320]{2,1,0:T(8,128)S(1)}, u32[]{:S(2)}, u32[]{:S(2)}) async-start(f32[16,8,320]{2,1,0:T(8,128)} %bitcast.8), calls=%async_computation | async-start | bytes 393216 | tf_op jit(solution)/shard_map/all_to_all | solution.py:329
  28.0 1.2 copy-start.4
  29.2 5.5 %copy-start.7 = (f32[1,3,8,8,8,128]{5,4,3,2,1,0:T(8,128)S(1)}, f32[1,3,8,8,8,128]{5,4,3,2,1,0:T(8,128)}, u32[]{:S(2)}) copy-start(f32[1,3,8,8,8,128]{5,4,3,2,1,0:T(8,128)} %param.13) | copy-start | bytes 2359300
  29.2 5.5 %copy-start.11 = (f32[1,8,8,8,128]{4,3,2,1,0:T(8,128)S(1)}, f32[1,8,8,8,128]{4,3,2,1,0:T(8,128)}, u32[]{:S(2)}) copy-start(f32[1,8,8,8,128]{4,3,2,1,0:T(8,128)} %param.14) | copy-start | bytes 786436
  29.2 5.5 %copy-start.12 = (f32[1,8,8,8,128]{4,3,2,1,0:T(8,128)S(1)}, f32[1,8,8,8,128]{4,3,2,1,0:T(8,128)}, u32[]{:S(2)}) copy-start(f32[1,8,8,8,128]{4,3,2,1,0:T(8,128)} %param.12) | copy-start | bytes 786436
  33.6 1.1 copy-start
  38.4 0.9 copy-start.5
  39.4 14.6 %all-to-all-start.1 = ((f32[16,8,320]{2,1,0:T(8,128)}), f32[16,8,320]{2,1,0:T(8,128)S(1)}, u32[]{:S(2)}, u32[]{:S(2)}) async-start(f32[16,8,320]{2,1,0:T(8,128)} %bitcast.14), calls=%async_computation.1 | async-start | bytes 393216 | tf_op jit(solution)/shard_map/all_to_all | solution.py:329
  54.0 1.2 copy-start.6
  55.2 4.4 %copy-start.1 = (f32[2560,128]{1,0:T(8,128)S(1)}, f32[2560,128]{1,0:T(8,128)}, u32[]{:S(2)}) copy-start(f32[2560,128]{1,0:T(8,128)} %copy-done) | copy-start | bytes 3932164
  55.2 4.4 %copy-start.8 = (f32[1,3,8,8,8,128]{5,4,3,2,1,0:T(8,128)S(1)}, f32[1,3,8,8,8,128]{5,4,3,2,1,0:T(8,128)}, u32[]{:S(2)}) copy-start(f32[1,3,8,8,8,128]{5,4,3,2,1,0:T(8,128)} %param.13) | copy-start | bytes 2359300
  55.2 4.4 %copy-start.9 = (f32[1,5,8,8,8,128]{5,4,3,2,1,0:T(8,128)S(1)}, f32[1,5,8,8,8,128]{5,4,3,2,1,0:T(8,128)}, u32[]{:S(2)}) copy-start(f32[1,5,8,8,8,128]{5,4,3,2,1,0:T(8,128)} %broadcast_multiply_fusion) | copy-start | bytes 3932164
  55.2 4.4 %copy-start.13 = (f32[1,8,8,8,128]{4,3,2,1,0:T(8,128)S(1)}, f32[1,8,8,8,128]{4,3,2,1,0:T(8,128)}, u32[]{:S(2)}) copy-start(f32[1,8,8,8,128]{4,3,2,1,0:T(8,128)} %param.12) | copy-start | bytes 786436
  85.8 4.4 %copy-start.10 = (f32[1,5,8,8,8,128]{5,4,3,2,1,0:T(8,128)S(1)}, f32[1,5,8,8,8,128]{5,4,3,2,1,0:T(8,128)}, u32[]{:S(2)}) copy-start(f32[1,5,8,8,8,128]{5,4,3,2,1,0:T(8,128)} %param.16) | copy-start | bytes 3932164

commit v2 on v1

--- a/solution.py
+++ b/solution.py
@@ -248,6 +248,66 @@
         scratch_shapes=[pltpu.VMEM(raw.shape, jnp.float32)],
         compiler_params=pltpu.CompilerParams(vmem_limit_bytes=40 << 20),
     )(state, raw, arrived, place, rolled)
+
+
+def exchange_kernel(buffer, arrived, landed, send_sem, recv_sem):
+    tiles = lax.axis_size("tile")
+    me = lax.axis_index("tile")
+    barrier = pltpu.get_barrier_semaphore()
+
+    def peer(offset):
+        return {"tile": lax.rem(me + offset, tiles)}
+
+    def copy(offset):
+        to = lax.rem(me + offset, tiles)
+        return pltpu.make_async_remote_copy(
+            src_ref=buffer.at[to],
+            dst_ref=landed.at[me],
+            send_sem=send_sem.at[offset],
+            recv_sem=recv_sem.at[offset],
+            device_id=peer(offset),
+            device_id_type=pl.DeviceIdType.MESH,
+        )
+
+    def greet(offset, carry):
+        pl.semaphore_signal(
+            barrier, inc=1, device_id=peer(offset), device_id_type=pl.DeviceIdType.MESH
+        )
+        return carry
+
+    def begin(offset, carry):
+        copy(offset).start()
+        return carry
+
+    def finish(offset, carry):
+        copy(offset).wait()
+        return carry
+
+    lax.fori_loop(1, tiles, greet, 0)
+    pl.semaphore_wait(barrier, tiles - 1)
+    lax.fori_loop(1, tiles, begin, 0)
+    landed[me] = jnp.zeros(landed.shape[1:], jnp.float32)
+    lax.fori_loop(1, tiles, finish, 0)
+    arrived[...] = landed[...]
+
+
+def exchanged(buffer, identifier):
+    tiles = lax.axis_size("tile")
+    blocks = buffer.reshape(tiles, -1, buffer.shape[1])
+    return pl.pallas_call(
+        exchange_kernel,
+        out_shape=jax.ShapeDtypeStruct(blocks.shape, jnp.float32),
+        in_specs=[VMEM],
+        out_specs=VMEM,
+        scratch_shapes=[
+            pltpu.VMEM(blocks.shape, jnp.float32),
+            pltpu.SemaphoreType.DMA((tiles,)),
+            pltpu.SemaphoreType.DMA((tiles,)),
+        ],
+        compiler_params=pltpu.CompilerParams(
+            collective_id=identifier, has_side_effects=True, vmem_limit_bytes=16 << 20
+        ),
+    )(blocks).reshape(buffer.shape)
 
 
 def turning():
@@ -326,7 +386,7 @@
     def rates(states):
         traced = [traces_of(state, masks, turn, inner, send) for state in states]
         buffer = jnp.concatenate([leave for raw, leave in traced], axis=1)
-        arrived = lax.all_to_all(buffer, "tile", split_axis=0, concat_axis=0, tiled=True)
+        arrived = exchanged(buffer, len(states) - 1)
         return [
             rate_of(state, raw, arrived[:, at * ROWS : (at + 1) * ROWS], place, rolled)
             for at, (state, (raw, leave)) in enumerate(zip(states, traced))
@@ -345,19 +405,24 @@
 
     state = start
     if levels == 2:
+        base = level == 0
         received = shifted(start, "level", 1)
-        own_rate = rates([state])[0]
-        received, own_rate = lax.optimization_barrier((received, own_rate))
-        lower = jnp.where(level == 0, start, received)
-        for repeat in range(TSTEPS):
-            if repeat == 0:
-                below = rates([lower])[0]
-            else:
-                own_rate, below = rates([state, lower])
-            state = advance(state, own_rate, older, old, below)
-            lower = lower + step_size * below
-            older = old
-            old = below
+        first = rates([start])[0]
+        ahead = start + step_size * first
+        second = rates([ahead])[0]
+        third_state = ahead + step_size * second
+        received, third_state = lax.optimization_barrier((received, third_state))
+        lower = jnp.where(base, third_state, received)
+        lower_first = rates([lower])[0]
+        last_below = shifted(lower_first, "level", 1)
+        state = advance(start, first, older, old, lower_first)
+        lower = lower + step_size * lower_first
+        own_second, lower_second = rates([state, lower])
+        state = advance(state, own_second, old, lower_first, lower_second)
+        own_third = rates([state])[0]
+        own_third, last_below = lax.optimization_barrier((own_third, last_below))
+        final = advance(state, own_third, lower_first, lower_second, last_below)
+        state = jnp.where(base, third_state + step_size * lower_first, final)
     else:
         for repeat in range(TSTEPS):
             own_rate = rates([state])[0]

time: 123 us -> 115 us (0.935)
  Pallas kernels: 44.9 us -> 95.3 us
  blocking collectives: 27.9 us -> 0 us
  waiting for transfers between devices: 15.1 us -> 0.01 us
  starting transfers between devices: 17.4 us -> 7.66 us
  local copies, waits for them, and re-layouts: 5.71 us -> 2.49 us
  other arithmetic: 9.7 us -> 8.23 us
    pallas_call x0 -> x5, Pallas kernels: none -> 49.1 us  [exchanged(): pl.pallas_call(exchange_kernel, out_shape=jax.ShapeDtypeStruct(blocks.sha...]
    all_to_all x2 -> x0, blocking collectives: 27.9 us -> none  [rates(): lax.all_to_all(buffer, 'tile', split_axis=0, concat_axis=0, tiled=True)]
    all_to_all x2 -> x0, waiting for transfers between devices: 15.1 us -> none  [rates(): lax.all_to_all(buffer, 'tile', split_axis=0, concat_axis=0, tiled=True)]
    all_to_all x2 -> x0, starting transfers between devices: 11.5 us -> none  [rates(): lax.all_to_all(buffer, 'tile', split_axis=0, concat_axis=0, tiled=True)]
    unnamed x40 -> x30, local copies, waits for them, and re-layouts: 5.43 us -> 2.3 us
    mul x1, other arithmetic: 2.57 us -> 0.19 us  [advance(): weight_back * older + weight_here * old + weight_next * below]
    ppermute x1 -> x2, starting transfers between devices: 5.91 us -> 7.66 us  [shifted(): return lax.ppermute(block, axis, route)]
    select_n x2, other arithmetic: 2.79 us -> 1.19 us  [advance(): return jnp.where(level == 0, state + step_size * own_rate, corrected)]
  transfers between devices with their start and end apart: 3 -> 2, of which waited for: 2 -> 0; matrix products, arithmetic and copies ran while one was open for 3% -> 4% of each run, Pallas kernels for 7% -> 69%
where the time goes in v2:
time: 115 us
  Pallas kernels  95.3 us (83%)
  other arithmetic  8.23 us (7%)
  starting transfers between devices  7.66 us (7%)
  local copies, waits for them, and re-layouts  2.49 us (2%)
    pallas_call x5, Pallas kernels, exchanged(): pl.pallas_call(exchange_kernel, out_shape=jax.ShapeDtypeStruct(blocks.sha...  49.1 us
    pallas_call x6, Pallas kernels, rate_of(): pl.pallas_call(rate_kernel, out_shape=jax.ShapeDtypeStruct(state.shape, j...  27.7 us
    pallas_call x6, Pallas kernels, traces_of(): pl.pallas_call(trace_kernel, out_shape=(jax.ShapeDtypeStruct((ROWS, slots...  18.4 us
    ppermute x2, starting transfers between devices, shifted(): return lax.ppermute(block, axis, route)  7.66 us
    concatenate x1, other arithmetic, body(): jnp.concatenate([density.reshape(-1, width), momentum.reshape(-1, width),...  2.47 us
    unnamed x30, local copies, waits for them, and re-layouts  2.3 us
  transfers between devices with their start and end apart: 2, of which 0 were waited for; matrix products, arithmetic and copies ran while one was open for 4% of the time, Pallas kernels for 69%

profile of v2, /device:TPU:0, one launch (start us, length us, event | category | flops | bytes accessed | tf_op | source)
XLA Modules:
  0.0 114.5 jit_solution(13585881975333807393)
XLA Ops:
  0.0 0.0 copy-start.9
  0.0 0.0 copy-start.12
  0.0 0.0 copy-start.10
  0.0 0.0 copy-start.14
  0.0 0.0 copy-start.13
  0.0 2.5 %pad_maximum_fusion.state = f32[2560,128]{1,0:T(8,128)} fusion(f32[512,128]{1,0:T(8,128)} %bitcast.76, f32[1536,128]{1,0:T(8,128)} %bitcast.71, f32[512,128]{1,0:T(8,128)} %bitcast.81), kind=kLoop, calls=%fused_computation.3 | loop fusion | flops 655360 | bytes 2621440 | tf_op jit(solution)/shard_map/concatenate | solution.py:341
  2.5 0.0 copy-start.2
  2.5 6.1 %collective-permute-start = (f32[2560,128]{1,0:T(8,128)}, f32[2560,128]{1,0:T(8,128)}, u32[]{:S(2)}, u32[]{:S(2)}) collective-permute-start(f32[2560,128]{1,0:T(8,128)} %pad_maximum_fusion.state), channel_id=1, source_target_pairs={{0,16},{1,17},{2,18},{3,19},{4,20},{5,21},{6,22},{7,23},{8,24},{9,... | collective-permute-start | bytes 3932168 | tf_op jit(solution)/shard_map/ppermute | solution.py:26
  8.5 0.0 copy-done.9
  8.6 0.0 copy-done.12
  8.6 0.0 copy-done.10
  8.6 0.0 copy-done.14
  8.7 0.2 convert_reduce_fusion
  8.8 0.0 copy-done.13
  8.9 0.3 convolution_convert_fusion.place
  9.2 0.3 convolution_convert_fusion.1.send
  9.4 0.5 fusion.1.inner
  9.9 0.0 copy-done.2
  9.9 0.0 copy-start.11
  10.0 4.2 %shard_map.118 = (f32[320,768]{1,0:T(8,128)S(1)}, f32[128,320]{1,0:T(8,128)S(1)}) custom-call(f32[2560,128]{1,0:T(8,128)} %pad_maximum_fusion.state, f32[8,768]{1,0:T(8,128)S(1)} %fusion.17.masks, bf16[64,256]{1,0:T(8,128)(2,1)S(1)} %copy-done.2, bf16[768,768]{1,0:T(8,128)(2,1)S(1)} %fusion.1.inner, bf16[128,768]{1,0:T(8,128)(2,1)S(1)} %convolution_convert_fusion.1.send), custom_call_target="tpu_custom_call" | custom-call | tf_op jit(solution)/shard_map/pallas_call | solution.py:229
  14.1 9.0 %shard_map.119 = f32[16,8,320]{2,1,0:T(8,128)S(1)} custom-call(f32[16,8,320]{2,1,0:T(8,128)S(1)} %bitcast.68), custom_call_target="tpu_custom_call" | custom-call | tf_op jit(solution)/shard_map/pallas_call | solution.py:297
  23.1 0.0 copy-done.11
  23.1 0.1 broadcast_in_dim.2.rolled
  23.2 0.0 copy-start.3
  23.2 0.0 copy-start.5
  23.2 0.0 copy-start.6
  23.2 5.8 %shard_map.120 = f32[2560,128]{1,0:T(8,128)S(1)} custom-call(f32[2560,128]{1,0:T(8,128)} %pad_maximum_fusion.state, f32[320,768]{1,0:T(8,128)S(1)} %get-tuple-element.21.raw, f32[128,320]{1,0:T(8,128)S(1)} %bitcast.63, bf16[128,768]{1,0:T(8,128)(2,1)S(1)} %convolution_convert_fusion.place, f32[8,8,128]{2,1,0:T(8,128)S(1)} %broadcast_in_dim.2.rolled), custom_call_target="tpu_custom_call" | custom-call | tf_op jit(solution)/shard_map/pallas_call | solution.py:243
  29.0 0.0 copy-done.3
  29.0 0.0 copy-done.5
  29.1 0.0 copy-done.6
  29.1 1.2 %multiply_add_fusion.1.state = f32[2560,128]{1,0:T(8,128)} fusion(f32[2560,128]{1,0:T(8,128)S(1)} %shard_map.120, f32[512,128]{1,0:T(8,128)S(1)} %bitcast.77, f32[1536,128]{1,0:T(8,128)S(1)} %bitcast.72, f32[512,128]{1,0:T(8,128)S(1)} %bitcast.82), kind=kLoop, calls=%fused_computation.21 | loop fusion | flops 1310720 | bytes 3932160 | tf_op jit(solution)/shard_map/add | solution.py:411
  30.3 1.3 %copy-done = f32[2560,128]{1,0:T(8,128)S(1)} copy-done((f32[2560,128]{1,0:T(8,128)S(1)}, f32[2560,128]{1,0:T(8,128)}, u32[]{:S(2)}) %copy-start) | copy-done | bytes 1310744
  31.6 2.9 %shard_map.121 = (f32[320,768]{1,0:T(8,128)S(1)}, f32[128,320]{1,0:T(8,128)S(1)}) custom-call(f32[2560,128]{1,0:T(8,128)S(1)} %copy-done, f32[8,768]{1,0:T(8,128)S(1)} %fusion.17.masks, bf16[64,256]{1,0:T(8,128)(2,1)S(1)} %copy-done.2, bf16[768,768]{1,0:T(8,128)(2,1)S(1)} %fusion.1.inner, bf16[128,768]{1,0:T(8,128)(2,1)S(1)} %convolution_convert_fusion.1.send), custom_call_target="tpu_custom_call" | custom-call | tf_op jit(solution)/shard_map/pallas_call | solution.py:229
  34.5 9.3 %shard_map.122 = f32[16,8,320]{2,1,0:T(8,128)S(1)} custom-call(f32[16,8,320]{2,1,0:T(8,128)S(1)} %bitcast.69), custom_call_target="tpu_custom_call" | custom-call | tf_op jit(solution)/shard_map/pallas_call | solution.py:297
  43.8 0.0 copy-done.1
  43.8 0.0 copy-start.8
  43.8 4.4 %shard_map.123 = f32[2560,128]{1,0:T(8,128)S(1)} custom-call(f32[2560,128]{1,0:T(8,128)S(1)} %copy-done.1, f32[320,768]{1,0:T(8,128)S(1)} %get-tuple-element.23.raw, f32[128,320]{1,0:T(8,128)S(1)} %bitcast.65, bf16[128,768]{1,0:T(8,128)(2,1)S(1)} %convolution_convert_fusion.place, f32[8,8,128]{2,1,0:T(8,128)S(1)} %broadcast_in_dim.2.rolled), custom_call_target="tpu_custom_call" | custom-call | tf_op jit(solution)/shard_map/pallas_call | solution.py:243
  48.2 0.0 copy-done.8
  48.2 0.0 copy-start.4
  48.3 0.2 broadcast_multiply_fusion
  48.5 0.9 copy-done.4
  49.4 0.3 multiply_add_fusion
  49.7 0.0 collective-permute-done
  49.7 0.1 broadcast_select_fusion.state
  49.8 2.8 %shard_map.124 = (f32[320,768]{1,0:T(8,128)S(1)}, f32[128,320]{1,0:T(8,128)S(1)}) custom-call(f32[2560,128]{1,0:T(8,128)S(1)} %broadcast_select_fusion.state, f32[8,768]{1,0:T(8,128)S(1)} %fusion.17.masks, bf16[64,256]{1,0:T(8,128)(2,1)S(1)} %copy-done.2, bf16[768,768]{1,0:T(8,128)(2,1)S(1)} %fusion.1.inner, bf16[128,768]{1,0:T(8,128)(2,1)S(1)} %convolution_convert_fusion.1.send), custom_call_target="tpu_custom_call" | custom-call | tf_op jit(solution)/shard_map/pallas_call | solution.py:229
  52.7 9.3 %shard_map.125 = f32[16,8,320]{2,1,0:T(8,128)S(1)} custom-call(f32[16,8,320]{2,1,0:T(8,128)S(1)} %bitcast.70), custom_call_target="tpu_custom_call" | custom-call | tf_op jit(solution)/shard_map/pallas_call | solution.py:297
  62.0 0.0 copy-start.7
  62.0 4.4 %shard_map.126 = f32[2560,128]{1,0:T(8,128)S(1)} custom-call(f32[2560,128]{1,0:T(8,128)S(1)} %broadcast_select_fusion.state, f32[320,768]{1,0:T(8,128)S(1)} %get-tuple-element.27.raw, f32[128,320]{1,0:T(8,128)S(1)} %bitcast.66, bf16[128,768]{1,0:T(8,128)(2,1)S(1)} %convolution_convert_fusion.place, f32[8,8,128]{2,1,0:T(8,128)S(1)} %broadcast_in_dim.2.rolled), custom_call_target="tpu_custom_call" | custom-call | tf_op jit(solution)/shard_map/pallas_call | solution.py:243
  66.4 1.6 %collective-permute-start.1 = (f32[2560,128]{1,0:T(8,128)S(1)}, f32[2560,128]{1,0:T(8,128)S(1)}, u32[]{:S(2)}, u32[]{:S(2)}) collective-permute-start(f32[2560,128]{1,0:T(8,128)S(1)} %shard_map.126), channel_id=1, source_target_pairs={{0,16},{1,17},{2,18},{3,19},{4,20},{5,21},{6,22},{7,23},{8,24},{9,... | collective-permute-start | bytes 3932168 | tf_op jit(solution)/shard_map/ppermute | solution.py:26
  68.0 0.0 copy-done.7
  68.1 0.6 fusion.5
  68.7 2.8 %shard_map.128 = (f32[320,768]{1,0:T(8,128)S(1)}, f32[128,320]{1,0:T(8,128)S(1)}) custom-call(f32[2560,128]{1,0:T(8,128)S(1)} %get-tuple-element.40.state, f32[8,768]{1,0:T(8,128)S(1)} %fusion.17.masks, bf16[64,256]{1,0:T(8,128)(2,1)S(1)} %copy-done.2, bf16[768,768]{1,0:T(8,128)(2,1)S(1)} %fusion.1.inner, bf16[128,768]{1,0:T(8,128)(2,1)S(1)} %convolution_convert_fusion.1.send), custom_call_target="tpu_custom_call" | custom-call | tf_op jit(solution)/shard_map/pallas_call | solution.py:229
  71.5 2.9 %shard_map.127 = (f32[320,768]{1,0:T(8,128)S(1)}, f32[128,320]{1,0:T(8,128)S(1)}) custom-call(f32[2560,128]{1,0:T(8,128)S(1)} %get-tuple-element.39.state, f32[8,768]{1,0:T(8,128)S(1)} %fusion.17.masks, bf16[64,256]{1,0:T(8,128)(2,1)S(1)} %copy-done.2, bf16[768,768]{1,0:T(8,128)(2,1)S(1)} %fusion.1.inner, bf16[128,768]{1,0:T(8,128)(2,1)S(1)} %convolution_convert_fusion.1.send), custom_call_target="tpu_custom_call" | custom-call | tf_op jit(solution)/shard_map/pallas_call | solution.py:229
  74.4 0.1 maximum_bitcast_fusion.buffer
  74.5 11.1 %shard_map.129 = f32[16,8,640]{2,1,0:T(8,128)S(1)} custom-call(f32[16,8,640]{2,1,0:T(8,128)S(1)} %maximum_bitcast_fusion.buffer), custom_call_target="tpu_custom_call" | custom-call | tf_op jit(solution)/shard_map/pallas_call | solution.py:297
  85.7 0.1 fusion.20
  85.8 4.4 %shard_map.131 = f32[2560,128]{1,0:T(8,128)S(1)} custom-call(f32[2560,128]{1,0:T(8,128)S(1)} %get-tuple-element.40.state, f32[320,768]{1,0:T(8,128)S(1)} %get-tuple-element.32.raw, f32[128,320]{1,0:T(8,128)S(1)} %get-tuple-element.42.arrived, bf16[128,768]{1,0:T(8,128)(2,1)S(1)} %convolution_convert_fusion.place, f32[8,8,128]{2,1,0:T(8,128)S(1)} %broadcast_in_dim.2.rolled), custom_call_target="tpu_custom_call" | custom-call | tf_op jit(solution)/shard_map/pallas_call | solution.py:243
  90.2 4.4 %shard_map.130 = f32[2560,128]{1,0:T(8,128)S(1)} custom-call(f32[2560,128]{1,0:T(8,128)S(1)} %get-tuple-element.39.state, f32[320,768]{1,0:T(8,128)S(1)} %get-tuple-element.29.raw, f32[128,320]{1,0:T(8,128)S(1)} %get-tuple-element.41.arrived, bf16[128,768]{1,0:T(8,128)(2,1)S(1)} %convolution_convert_fusion.place, f32[8,8,128]{2,1,0:T(8,128)S(1)} %broadcast_in_dim.2.rolled), custom_call_target="tpu_custom_call" | custom-call | tf_op jit(solution)/shard_map/pallas_call | solution.py:243
  94.6 0.6 fusion.12.state
  95.1 2.8 %shard_map.132 = (f32[320,768]{1,0:T(8,128)S(1)}, f32[128,320]{1,0:T(8,128)S(1)}) custom-call(f32[2560,128]{1,0:T(8,128)S(1)} %fusion.12.state, f32[8,768]{1,0:T(8,128)S(1)} %fusion.17.masks, bf16[64,256]{1,0:T(8,128)(2,1)S(1)} %copy-done.2, bf16[768,768]{1,0:T(8,128)(2,1)S(1)} %fusion.1.inner, bf16[128,768]{1,0:T(8,128)(2,1)S(1)} %convolution_convert_fusion.1.send), custom_call_target="tpu_custom_call" | custom-call | tf_op jit(solution)/shard_map/pallas_call | solution.py:229
  98.0 10.3 %shard_map.133 = f32[16,8,320]{2,1,0:T(8,128)S(1)} custom-call(f32[16,8,320]{2,1,0:T(8,128)S(1)} %bitcast.67), custom_call_target="tpu_custom_call" | custom-call | tf_op jit(solution)/shard_map/pallas_call | solution.py:297
  108.3 4.4 %shard_map.134 = f32[2560,128]{1,0:T(8,128)S(1)} custom-call(f32[2560,128]{1,0:T(8,128)S(1)} %fusion.12.state, f32[320,768]{1,0:T(8,128)S(1)} %get-tuple-element.33.raw, f32[128,320]{1,0:T(8,128)S(1)} %bitcast.64, bf16[128,768]{1,0:T(8,128)(2,1)S(1)} %convolution_convert_fusion.place, f32[8,8,128]{2,1,0:T(8,128)S(1)} %broadcast_in_dim.2.rolled), custom_call_target="tpu_custom_call" | custom-call | tf_op jit(solution)/shard_map/pallas_call | solution.py:243
  112.7 0.0 collective-permute-done.1
  112.7 1.9 %subtract_multiply_fusion = f32[2560,128]{1,0:T(8,128)} fusion(f32[2560,128]{1,0:T(8,128)S(1)} %collective-permute-done.1, f32[2560,128]{1,0:T(8,128)S(1)} %shard_map.131, f32[2560,128]{1,0:T(8,128)S(1)} %shard_map.126, f32[2560,128]{1,0:T(8,128)S(1)} %fusion.12.state, f32[2560,128]{1,0:T(8,128)S(1)} %shard_map.134, f32[2560,128]{1,0:T(8,128)S(1)} %multiply_add_fusion, ...), kind=kLoop, calls=%fused_computation.19 | loop fusion | flops 6553600 | bytes 10485761 | tf_op jit(solution)/shard_map/div | solution.py:433
  (7 shorter events, 0.1 us)
Async XLA Ops:
  0.0 8.5 %copy-start.9 = (s32[1,768]{1,0:T(1,128)S(1)}, s32[1,768]{1,0:T(1,128)}, u32[]{:S(2)}) copy-start(s32[1,768]{1,0:T(1,128)} %param.20) | copy-start | bytes 9220
  0.0 8.6 %copy-start.12 = (s32[1,768]{1,0:T(1,128)S(1)}, s32[1,768]{1,0:T(1,128)}, u32[]{:S(2)}) copy-start(s32[1,768]{1,0:T(1,128)} %param.21) | copy-start | bytes 9220
  0.0 8.6 %copy-start.10 = (s32[1,120]{1,0:T(1,128)S(1)}, s32[1,120]{1,0:T(1,128)}, u32[]{:S(2)}) copy-start(s32[1,120]{1,0:T(1,128)} %param.17) | copy-start | bytes 1444
  0.0 8.6 %copy-start.14 = (s32[1,120]{1,0:T(1,128)S(1)}, s32[1,120]{1,0:T(1,128)}, u32[]{:S(2)}) copy-start(s32[1,120]{1,0:T(1,128)} %param.18) | copy-start | bytes 1444
  0.0 8.8 %copy-start.13 = (s32[1,120]{1,0:T(1,128)S(1)}, s32[1,120]{1,0:T(1,128)}, u32[]{:S(2)}) copy-start(s32[1,120]{1,0:T(1,128)} %param.19) | copy-start | bytes 1444
  2.5 7.4 %copy-start.2 = (bf16[64,256]{1,0:T(8,128)(2,1)S(1)}, bf16[64,256]{1,0:T(8,128)(2,1)}, u32[]{:S(2)}) copy-start(bf16[64,256]{1,0:T(8,128)(2,1)} %constant.25.clone.turn) | copy-start | bytes 98308
  2.5 47.2 %collective-permute-start = (f32[2560,128]{1,0:T(8,128)}, f32[2560,128]{1,0:T(8,128)}, u32[]{:S(2)}, u32[]{:S(2)}) collective-permute-start(f32[2560,128]{1,0:T(8,128)} %pad_maximum_fusion.state), channel_id=1, source_target_pairs={{0,16},{1,17},{2,18},{3,19},{4,20},{5,21},{6,22},{7,23},{8,24},{9,... | collective-permute-start | bytes 3932168 | tf_op jit(solution)/shard_map/ppermute | solution.py:26
  9.9 13.2 %copy-start.11 = (f32[8,8]{1,0:T(8,128)S(1)}, f32[8,8]{1,0:T(8,128)}, u32[]{:S(2)}) copy-start(f32[8,8]{1,0:T(8,128)} %constant.26.clone) | copy-start | bytes 772
  23.2 5.8 %copy-start.3 = (f32[1,3,8,8,8,128]{5,4,3,2,1,0:T(8,128)S(1)}, f32[1,3,8,8,8,128]{5,4,3,2,1,0:T(8,128)}, u32[]{:S(2)}) copy-start(f32[1,3,8,8,8,128]{5,4,3,2,1,0:T(8,128)} %param.13) | copy-start | bytes 2359300
  23.2 5.8 %copy-start.5 = (f32[1,8,8,8,128]{4,3,2,1,0:T(8,128)S(1)}, f32[1,8,8,8,128]{4,3,2,1,0:T(8,128)}, u32[]{:S(2)}) copy-start(f32[1,8,8,8,128]{4,3,2,1,0:T(8,128)} %param.14) | copy-start | bytes 786436
  23.2 5.8 %copy-start.6 = (f32[1,8,8,8,128]{4,3,2,1,0:T(8,128)S(1)}, f32[1,8,8,8,128]{4,3,2,1,0:T(8,128)}, u32[]{:S(2)}) copy-start(f32[1,8,8,8,128]{4,3,2,1,0:T(8,128)} %param.12) | copy-start | bytes 786436
  30.3 1.3 %copy-start = (f32[2560,128]{1,0:T(8,128)S(1)}, f32[2560,128]{1,0:T(8,128)}, u32[]{:S(2)}) copy-start(f32[2560,128]{1,0:T(8,128)} %multiply_add_fusion.1.state) | copy-start | bytes 3932164
  31.6 12.2 %copy-start.1 = (f32[2560,128]{1,0:T(8,128)S(1)}, f32[2560,128]{1,0:T(8,128)}, u32[]{:S(2)}) copy-start(f32[2560,128]{1,0:T(8,128)} %multiply_add_fusion.1.state) | copy-start | bytes 3932164
  43.8 4.4 %copy-start.8 = (f32[1,5,8,8,8,128]{5,4,3,2,1,0:T(8,128)S(1)}, f32[1,5,8,8,8,128]{5,4,3,2,1,0:T(8,128)}, u32[]{:S(2)}) copy-start(f32[1,5,8,8,8,128]{5,4,3,2,1,0:T(8,128)} %param.15) | copy-start | bytes 3932164
  48.2 1.1 copy-start.4
  62.0 6.0 %copy-start.7 = (f32[1,5,8,8,8,128]{5,4,3,2,1,0:T(8,128)S(1)}, f32[1,5,8,8,8,128]{5,4,3,2,1,0:T(8,128)}, u32[]{:S(2)}) copy-start(f32[1,5,8,8,8,128]{5,4,3,2,1,0:T(8,128)} %param.16) | copy-start | bytes 3932164
  66.4 46.2 %collective-permute-start.1 = (f32[2560,128]{1,0:T(8,128)S(1)}, f32[2560,128]{1,0:T(8,128)S(1)}, u32[]{:S(2)}, u32[]{:S(2)}) collective-permute-start(f32[2560,128]{1,0:T(8,128)S(1)} %shard_map.126), channel_id=1, source_target_pairs={{0,16},{1,17},{2,18},{3,19},{4,20},{5,21},{6,22},{7,23},{8,24},{9,... | collective-permute-start | bytes 3932168 | tf_op jit(solution)/shard_map/ppermute | solution.py:26

commit v3 on v2

--- a/solution.py
+++ b/solution.py
@@ -1,3 +1,5 @@
+import functools
+
 import jax
 import jax.numpy as jnp
 import numpy as np
@@ -109,7 +111,7 @@
     return ref[pl.ds(base + end, NODES, stride=NP), :]
 
 
-def trace_kernel(state, masks, turn, inner, send, raw, buffer, turned):
+def gather_traces(state, masks, turn, turned):
     width = state.shape[1]
     for which in range(6):
         lanes = pl.ds(which * width, width)
@@ -120,29 +122,38 @@
                 stacked = jnp.concatenate([(wide * m).astype(jnp.bfloat16) for m in mask], axis=0)
                 out = jnp.dot(turn[...], stacked, preferred_element_type=jnp.float32)
                 turned[at, pl.ds(v * NODES, NODES), lanes] = out.astype(jnp.bfloat16)
-    total = None
+
+
+def outgoing_of(turned, send):
     outgoing = None
     for at in range(3):
-        block = turned[at]
-        part = jnp.dot(block, inner[...], preferred_element_type=jnp.float32)
         leave = lax.dot_general(
-            send[...], block, (((1,), (1,)), ((), ())), preferred_element_type=jnp.float32
-        )
+            send[...], turned[at], (((1,), (1,)), ((), ())), preferred_element_type=jnp.float32
+        )
+        outgoing = leave if outgoing is None else outgoing + leave
+    return outgoing
+
+
+def inner_of(turned, inner):
+    total = None
+    for at in range(3):
+        part = jnp.dot(turned[at], inner[...], preferred_element_type=jnp.float32)
         total = part if total is None else total + part
-        outgoing = leave if outgoing is None else outgoing + leave
-    raw[...] = total
-    buffer[...] = outgoing
-
-
-def rate_kernel(state, raw, arrived, place, rolled, rate, view):
-    width = state.shape[1]
+    return total
+
+
+def outer_of(arrived, place):
+    total = None
+    for piece in pieces_of(arrived):
+        part = lax.dot_general(
+            piece, place[...], (((0,), (0,)), ((), ())), preferred_element_type=jnp.float32
+        )
+        total = part if total is None else total + part
+    return total
+
+
+def volume_of(state, rolled, rate):
     numbers = derivative_numbers()
-    total = raw[...]
-    for piece in pieces_of(arrived[...]):
-        total = total + lax.dot_general(
-            piece, place[...], (((0,), (0,)), ((), ())), preferred_element_type=jnp.float32
-        )
-    view[...] = total
 
     def combine(fields, target):
         result = None
@@ -190,6 +201,9 @@
     lax.fori_loop(0, NP, along_first, 0)
     lax.fori_loop(0, NP, along_second, 0)
 
+
+def lift_faces(state, view, rate):
+    width = state.shape[1]
     for which in range(6):
         direction, end = face_rows(which)
         normal = 2.0 * (which % 2) - 1.0
@@ -224,33 +238,11 @@
 VMEM = pl.BlockSpec(memory_space=pltpu.VMEM)
 
 
-def traces_of(state, masks, turn, inner, send):
-    slots = masks.shape[1]
-    return pl.pallas_call(
-        trace_kernel,
-        out_shape=(
-            jax.ShapeDtypeStruct((ROWS, slots), jnp.float32),
-            jax.ShapeDtypeStruct((send.shape[0], ROWS), jnp.float32),
-        ),
-        in_specs=[VMEM] * 5,
-        out_specs=(VMEM, VMEM),
-        scratch_shapes=[pltpu.VMEM((3, ROWS, slots), jnp.bfloat16)],
-        compiler_params=pltpu.CompilerParams(vmem_limit_bytes=40 << 20),
-    )(state, masks, turn, inner, send)
-
-
-def rate_of(state, raw, arrived, place, rolled):
-    return pl.pallas_call(
-        rate_kernel,
-        out_shape=jax.ShapeDtypeStruct(state.shape, jnp.float32),
-        in_specs=[VMEM] * 5,
-        out_specs=VMEM,
-        scratch_shapes=[pltpu.VMEM(raw.shape, jnp.float32)],
-        compiler_params=pltpu.CompilerParams(vmem_limit_bytes=40 << 20),
-    )(state, raw, arrived, place, rolled)
-
-
-def exchange_kernel(buffer, arrived, landed, send_sem, recv_sem):
+def rate_kernel(count, *refs):
+    states, refs = refs[:count], refs[count:]
+    masks, turn, inner, send, place, rolled = refs[:6]
+    rates, refs = refs[6 : 6 + count], refs[6 + count :]
+    turned, views, buffer, landed, send_sem, recv_sem = refs
     tiles = lax.axis_size("tile")
     me = lax.axis_index("tile")
     barrier = pltpu.get_barrier_semaphore()
@@ -259,9 +251,8 @@
         return {"tile": lax.rem(me + offset, tiles)}
 
     def copy(offset):
-        to = lax.rem(me + offset, tiles)
         return pltpu.make_async_remote_copy(
-            src_ref=buffer.at[to],
+            src_ref=buffer.at[lax.rem(me + offset, tiles)],
             dst_ref=landed.at[me],
             send_sem=send_sem.at[offset],
             recv_sem=recv_sem.at[offset],
@@ -284,30 +275,45 @@
         return carry
 
     lax.fori_loop(1, tiles, greet, 0)
+    for at in range(count):
+        gather_traces(states[at], masks, turn, turned.at[at])
+        leave = outgoing_of(turned.at[at], send)
+        buffer[:, at * FCAP : (at + 1) * FCAP, :] = leave.reshape(tiles, FCAP, ROWS)
     pl.semaphore_wait(barrier, tiles - 1)
     lax.fori_loop(1, tiles, begin, 0)
     landed[me] = jnp.zeros(landed.shape[1:], jnp.float32)
+    for at in range(count):
+        views[at] = inner_of(turned.at[at], inner)
+        volume_of(states[at], rolled, rates[at])
     lax.fori_loop(1, tiles, finish, 0)
-    arrived[...] = landed[...]
-
-
-def exchanged(buffer, identifier):
+    for at in range(count):
+        arrived = landed[:, at * FCAP : (at + 1) * FCAP, :].reshape(tiles * FCAP, ROWS)
+        views[at] = views[at] + outer_of(arrived, place)
+        lift_faces(states[at], views.at[at], rates[at])
+
+
+def rates_of(states, tables):
     tiles = lax.axis_size("tile")
-    blocks = buffer.reshape(tiles, -1, buffer.shape[1])
+    count = len(states)
+    slots = tables[0].shape[1]
+    like = jax.ShapeDtypeStruct(states[0].shape, jnp.float32)
     return pl.pallas_call(
-        exchange_kernel,
-        out_shape=jax.ShapeDtypeStruct(blocks.shape, jnp.float32),
-        in_specs=[VMEM],
-        out_specs=VMEM,
+        functools.partial(rate_kernel, count),
+        out_shape=[like] * count,
+        in_specs=[VMEM] * (count + len(tables)),
+        out_specs=[VMEM] * count,
         scratch_shapes=[
-            pltpu.VMEM(blocks.shape, jnp.float32),
+            pltpu.VMEM((count, 3, ROWS, slots), jnp.bfloat16),
+            pltpu.VMEM((count, ROWS, slots), jnp.float32),
+            pltpu.VMEM((tiles, count * FCAP, ROWS), jnp.float32),
+            pltpu.VMEM((tiles, count * FCAP, ROWS), jnp.float32),
             pltpu.SemaphoreType.DMA((tiles,)),
             pltpu.SemaphoreType.DMA((tiles,)),
         ],
         compiler_params=pltpu.CompilerParams(
-            collective_id=identifier, has_side_effects=True, vmem_limit_bytes=16 << 20
+            collective_id=count - 1, has_side_effects=True, vmem_limit_bytes=40 << 20
         ),
-    )(blocks).reshape(buffer.shape)
+    )(*states, *tables)
 
 
 def turning():
@@ -383,14 +389,10 @@
     ).astype(np.float32)
     rolled = jnp.broadcast_to(jnp.asarray(diagonals)[:, :, None], (NP, NP, width))
 
+    tables = (masks, turn, inner, send, place, rolled)
+
     def rates(states):
-        traced = [traces_of(state, masks, turn, inner, send) for state in states]
-        buffer = jnp.concatenate([leave for raw, leave in traced], axis=1)
-        arrived = exchanged(buffer, len(states) - 1)
-        return [
-            rate_of(state, raw, arrived[:, at * ROWS : (at + 1) * ROWS], place, rolled)
-            for at, (state, (raw, leave)) in enumerate(zip(states, traced))
-        ]
+        return rates_of(states, tables)
 
     older = rhs_older.reshape(-1, width)
     old = rhs_old.reshape(-1, width)

time: 115 us -> 84.9 us (0.74)
  Pallas kernels: 95.3 us -> 63.1 us
  starting transfers between devices: 7.66 us -> 9.9 us
    pallas_call x17 -> x5, Pallas kernels: 95.3 us -> 63.1 us  [rates_of(): pl.pallas_call(functools.partial(rate_kernel, count), out_shape=[like] *...]
    ppermute x2, starting transfers between devices: 7.66 us -> 9.9 us  [shifted(): return lax.ppermute(block, axis, route)]
    unnamed x30 -> x28, local copies, waits for them, and re-layouts: 2.3 us -> 2.3 us
  transfers between devices with their start and end apart: 2 -> 2, of which waited for: 0 -> 0; matrix products, arithmetic and copies ran while one was open for 4% -> 5% of each run, Pallas kernels for 69% -> 61%
where the time goes in v3:
time: 84.9 us; the launch traced here: 84.6 us
  Pallas kernels  63.1 us (74%)
  starting transfers between devices  9.9 us (12%)
  other arithmetic  8.36 us (10%)
  local copies, waits for them, and re-layouts  2.37 us (3%)
    pallas_call x5, Pallas kernels, rates_of(): pl.pallas_call(functools.partial(rate_kernel, count), out_shape=[like] *...  63.1 us
    ppermute x2, starting transfers between devices, shifted(): return lax.ppermute(block, axis, route)  9.9 us
    concatenate x1, other arithmetic, body(): jnp.concatenate([density.reshape(-1, width), momentum.reshape(-1, width),...  2.47 us
    unnamed x28, local copies, waits for them, and re-layouts  2.3 us
    div x1, other arithmetic, body(): return ((state - start) / (TSTEPS * step_size)).reshape(rhs_old.shape)  1.86 us
  transfers between devices with their start and end apart: 2, of which 0 were waited for; matrix products, arithmetic and copies ran while one was open for 5% of the time, Pallas kernels for 61%

profile of v3, /device:TPU:0, one launch (start us, length us, event | category | flops | bytes accessed | tf_op | source)
XLA Modules:
  0.0 84.6 jit_solution(3173311984028192755)
XLA Ops:
  0.0 0.0 copy-start.8
  0.0 0.0 copy-start.11
  0.0 0.0 copy-start.9
  0.0 0.0 copy-start.13
  0.0 0.0 copy-start.12
  0.0 2.5 %pad_maximum_fusion.refs_0_ = f32[2560,128]{1,0:T(8,128)} fusion(f32[512,128]{1,0:T(8,128)} %bitcast.56, f32[1536,128]{1,0:T(8,128)} %bitcast.51, f32[512,128]{1,0:T(8,128)} %bitcast.61), kind=kLoop, calls=%fused_computation.3 | loop fusion | flops 655360 | bytes 2621440 | tf_op jit(solution)/shard_map/concatenate | solution.py:347
  2.5 0.0 copy-start.10
  2.5 0.0 copy-start.1
  2.5 6.0 %collective-permute-start = (f32[2560,128]{1,0:T(8,128)}, f32[2560,128]{1,0:T(8,128)}, u32[]{:S(2)}, u32[]{:S(2)}) collective-permute-start(f32[2560,128]{1,0:T(8,128)} %pad_maximum_fusion.refs_0_), channel_id=1, source_target_pairs={{0,16},{1,17},{2,18},{3,19},{4,20},{5,21},{6,22},{7,23},{8,24},{9,... | collective-permute-start | bytes 3932168 | tf_op jit(solution)/shard_map/ppermute | solution.py:28
  8.5 0.0 copy-done.8
  8.6 0.0 copy-done.11
  8.6 0.0 copy-done.9
  8.6 0.0 copy-done.13
  8.6 0.2 convert_reduce_fusion
  8.8 0.0 copy-done.12
  8.8 0.3 convolution_convert_fusion.refs_5_.refs_6_
  9.1 0.3 convolution_convert_fusion.1.refs_4_.refs_5_
  9.4 0.5 fusion.1.refs_3_.refs_4_
  9.9 0.0 copy-done.10
  9.9 0.1 broadcast_in_dim.2.refs_6_.refs_7_
  10.0 0.0 copy-done.1
  10.0 0.0 copy-start.2
  10.0 0.0 copy-start.4
  10.0 0.0 copy-start.5
  10.0 12.1 %shard_map.118 = f32[2560,128]{1,0:T(8,128)S(1)} custom-call(f32[2560,128]{1,0:T(8,128)} %pad_maximum_fusion.refs_0_, f32[8,768]{1,0:T(8,128)S(1)} %fusion.17.refs_1_.refs_2_, bf16[64,256]{1,0:T(8,128)(2,1)S(1)} %copy-done.1, bf16[768,768]{1,0:T(8,128)(2,1)S(1)} %fusion.1.refs_3_.refs_4_, bf16[128,768]{1,0:T(8,128)(2,1)S(1)} %convolution_convert_fusion.1.refs_4_.refs_5_, ...), custom_call_target="tpu_custom_call" | custom-call | tf_op jit(solution)/shard_map/pallas_call | solution.py:300
  22.2 0.0 copy-done.2
  22.2 0.0 copy-done.4
  22.2 0.0 copy-done.5
  22.2 1.2 %multiply_add_fusion.1.refs_0_ = f32[2560,128]{1,0:T(8,128)} fusion(f32[2560,128]{1,0:T(8,128)S(1)} %shard_map.118, f32[512,128]{1,0:T(8,128)S(1)} %bitcast.57, f32[1536,128]{1,0:T(8,128)S(1)} %bitcast.52, f32[512,128]{1,0:T(8,128)S(1)} %bitcast.62), kind=kLoop, calls=%fused_computation.21 | loop fusion | flops 1310720 | bytes 3932160 | tf_op jit(solution)/shard_map/add | solution.py:413
  23.4 0.0 copy-start
  23.4 1.3 %copy-done = f32[2560,128]{1,0:T(8,128)S(1)} copy-done((f32[2560,128]{1,0:T(8,128)S(1)}, f32[2560,128]{1,0:T(8,128)}, u32[]{:S(2)}) %copy-start) | copy-done | bytes 1310744
  24.8 0.0 copy-start.7
  24.8 11.0 %shard_map.119 = f32[2560,128]{1,0:T(8,128)S(1)} custom-call(f32[2560,128]{1,0:T(8,128)S(1)} %copy-done, f32[8,768]{1,0:T(8,128)S(1)} %fusion.17.refs_1_.refs_2_, bf16[64,256]{1,0:T(8,128)(2,1)S(1)} %copy-done.1, bf16[768,768]{1,0:T(8,128)(2,1)S(1)} %fusion.1.refs_3_.refs_4_, bf16[128,768]{1,0:T(8,128)(2,1)S(1)} %convolution_convert_fusion.1.refs_4_.refs_5_, ...), custom_call_target="tpu_custom_call" | custom-call | tf_op jit(solution)/shard_map/pallas_call | solution.py:300
  35.8 0.0 copy-done.7
  35.8 0.0 copy-start.3
  35.8 0.2 broadcast_multiply_fusion
  36.0 0.9 %copy-done.3 = f32[1,3,8,8,8,128]{5,4,3,2,1,0:T(8,128)S(1)} copy-done((f32[1,3,8,8,8,128]{5,4,3,2,1,0:T(8,128)S(1)}, f32[1,3,8,8,8,128]{5,4,3,2,1,0:T(8,128)}, u32[]{:S(2)}) %copy-start.3) | copy-done | bytes 786456
  37.0 0.3 multiply_add_fusion
  37.3 0.0 collective-permute-done
  37.3 0.2 broadcast_select_fusion.refs_0_
  37.5 0.0 copy-start.6
  37.5 11.2 %shard_map.120 = f32[2560,128]{1,0:T(8,128)S(1)} custom-call(f32[2560,128]{1,0:T(8,128)S(1)} %broadcast_select_fusion.refs_0_, f32[8,768]{1,0:T(8,128)S(1)} %fusion.17.refs_1_.refs_2_, bf16[64,256]{1,0:T(8,128)(2,1)S(1)} %copy-done.1, bf16[768,768]{1,0:T(8,128)(2,1)S(1)} %fusion.1.refs_3_.refs_4_, ...), custom_call_target="tpu_custom_call" | custom-call | tf_op jit(solution)/shard_map/pallas_call | solution.py:300
  48.7 3.9 %collective-permute-start.1 = (f32[2560,128]{1,0:T(8,128)S(1)}, f32[2560,128]{1,0:T(8,128)S(1)}, u32[]{:S(2)}, u32[]{:S(2)}) collective-permute-start(f32[2560,128]{1,0:T(8,128)S(1)} %shard_map.120), channel_id=1, source_target_pairs={{0,16},{1,17},{2,18},{3,19},{4,20},{5,21},{6,22},{7,23},{8,24},{9,... | collective-permute-start | bytes 3932168 | tf_op jit(solution)/shard_map/ppermute | solution.py:28
  52.5 0.0 copy-done.6
  52.6 0.7 multiply_add_fusion.2
  53.2 17.8 %shard_map.121 = (f32[2560,128]{1,0:T(8,128)S(1)}, f32[2560,128]{1,0:T(8,128)S(1)}) custom-call(f32[2560,128]{1,0:T(8,128)S(1)} %get-tuple-element.20.refs_0_, f32[2560,128]{1,0:T(8,128)S(1)} %get-tuple-element.19.refs_1_, f32[8,768]{1,0:T(8,128)S(1)} %fusion.17.refs_1_.refs_2_, bf16[64,256]{1,0:T(8,128)(2,1)S(1)} %copy-done.1, ...), custom_call_target="tpu_custom_call" | custom-call | tf_op jit(solution)/shard_map/pallas_call | solution.py:300
  71.0 0.7 fusion.12.refs_0_
  71.7 11.0 %shard_map.122 = f32[2560,128]{1,0:T(8,128)S(1)} custom-call(f32[2560,128]{1,0:T(8,128)S(1)} %fusion.12.refs_0_, f32[8,768]{1,0:T(8,128)S(1)} %fusion.17.refs_1_.refs_2_, bf16[64,256]{1,0:T(8,128)(2,1)S(1)} %copy-done.1, bf16[768,768]{1,0:T(8,128)(2,1)S(1)} %fusion.1.refs_3_.refs_4_, bf16[128,768]{1,0:T(8,128)(2,1)S(1)} %convolution_convert_fusion.1.refs_4_.refs_5_, ...), custom_call_target="tpu_custom_call" | custom-call | tf_op jit(solution)/shard_map/pallas_call | solution.py:300
  82.7 0.0 collective-permute-done.1
  82.7 1.9 %subtract_multiply_fusion = f32[2560,128]{1,0:T(8,128)} fusion(f32[2560,128]{1,0:T(8,128)S(1)} %collective-permute-done.1, f32[2560,128]{1,0:T(8,128)S(1)} %get-tuple-element.14, f32[2560,128]{1,0:T(8,128)S(1)} %shard_map.120, f32[2560,128]{1,0:T(8,128)S(1)} %fusion.12.refs_0_, f32[2560,128]{1,0:T(8,128)S(1)} %shard_map.122, ...), kind=kLoop, calls=%fused_computation.19 | loop fusion | flops 6553600 | bytes 10485761 | tf_op jit(solution)/shard_map/div | solution.py:435
  (5 shorter events, 0.1 us)
Async XLA Ops:
  0.0 8.5 %copy-start.8 = (s32[1,768]{1,0:T(1,128)S(1)}, s32[1,768]{1,0:T(1,128)}, u32[]{:S(2)}) copy-start(s32[1,768]{1,0:T(1,128)} %param.20) | copy-start | bytes 9220
  0.0 8.6 %copy-start.11 = (s32[1,768]{1,0:T(1,128)S(1)}, s32[1,768]{1,0:T(1,128)}, u32[]{:S(2)}) copy-start(s32[1,768]{1,0:T(1,128)} %param.21) | copy-start | bytes 9220
  0.0 8.6 %copy-start.9 = (s32[1,120]{1,0:T(1,128)S(1)}, s32[1,120]{1,0:T(1,128)}, u32[]{:S(2)}) copy-start(s32[1,120]{1,0:T(1,128)} %param.17) | copy-start | bytes 1444
  0.0 8.6 %copy-start.13 = (s32[1,120]{1,0:T(1,128)S(1)}, s32[1,120]{1,0:T(1,128)}, u32[]{:S(2)}) copy-start(s32[1,120]{1,0:T(1,128)} %param.18) | copy-start | bytes 1444
  0.0 8.8 %copy-start.12 = (s32[1,120]{1,0:T(1,128)S(1)}, s32[1,120]{1,0:T(1,128)}, u32[]{:S(2)}) copy-start(s32[1,120]{1,0:T(1,128)} %param.19) | copy-start | bytes 1444
  2.5 7.4 %copy-start.10 = (f32[8,8]{1,0:T(8,128)S(1)}, f32[8,8]{1,0:T(8,128)}, u32[]{:S(2)}) copy-start(f32[8,8]{1,0:T(8,128)} %constant.26.clone) | copy-start | bytes 772
  2.5 7.5 %copy-start.1 = (bf16[64,256]{1,0:T(8,128)(2,1)S(1)}, bf16[64,256]{1,0:T(8,128)(2,1)}, u32[]{:S(2)}) copy-start(bf16[64,256]{1,0:T(8,128)(2,1)} %constant.25.clone.refs_2_.refs_3_) | copy-start | bytes 98308
  2.5 34.8 %collective-permute-start = (f32[2560,128]{1,0:T(8,128)}, f32[2560,128]{1,0:T(8,128)}, u32[]{:S(2)}, u32[]{:S(2)}) collective-permute-start(f32[2560,128]{1,0:T(8,128)} %pad_maximum_fusion.refs_0_), channel_id=1, source_target_pairs={{0,16},{1,17},{2,18},{3,19},{4,20},{5,21},{6,22},{7,23},{8,24},{9,... | collective-permute-start | bytes 3932168 | tf_op jit(solution)/shard_map/ppermute | solution.py:28
  10.0 12.2 %copy-start.2 = (f32[1,3,8,8,8,128]{5,4,3,2,1,0:T(8,128)S(1)}, f32[1,3,8,8,8,128]{5,4,3,2,1,0:T(8,128)}, u32[]{:S(2)}) copy-start(f32[1,3,8,8,8,128]{5,4,3,2,1,0:T(8,128)} %param.13) | copy-start | bytes 2359300
  10.0 12.2 %copy-start.4 = (f32[1,8,8,8,128]{4,3,2,1,0:T(8,128)S(1)}, f32[1,8,8,8,128]{4,3,2,1,0:T(8,128)}, u32[]{:S(2)}) copy-start(f32[1,8,8,8,128]{4,3,2,1,0:T(8,128)} %param.14) | copy-start | bytes 786436
  10.0 12.2 %copy-start.5 = (f32[1,8,8,8,128]{4,3,2,1,0:T(8,128)S(1)}, f32[1,8,8,8,128]{4,3,2,1,0:T(8,128)}, u32[]{:S(2)}) copy-start(f32[1,8,8,8,128]{4,3,2,1,0:T(8,128)} %param.12) | copy-start | bytes 786436
  23.4 1.3 %copy-start = (f32[2560,128]{1,0:T(8,128)S(1)}, f32[2560,128]{1,0:T(8,128)}, u32[]{:S(2)}) copy-start(f32[2560,128]{1,0:T(8,128)} %multiply_add_fusion.1.refs_0_) | copy-start | bytes 3932164
  24.8 11.0 %copy-start.7 = (f32[1,5,8,8,8,128]{5,4,3,2,1,0:T(8,128)S(1)}, f32[1,5,8,8,8,128]{5,4,3,2,1,0:T(8,128)}, u32[]{:S(2)}) copy-start(f32[1,5,8,8,8,128]{5,4,3,2,1,0:T(8,128)} %param.15) | copy-start | bytes 3932164
  35.8 1.1 %copy-start.3 = (f32[1,3,8,8,8,128]{5,4,3,2,1,0:T(8,128)S(1)}, f32[1,3,8,8,8,128]{5,4,3,2,1,0:T(8,128)}, u32[]{:S(2)}) copy-start(f32[1,3,8,8,8,128]{5,4,3,2,1,0:T(8,128)} %param.13) | copy-start | bytes 2359300
  37.5 15.1 %copy-start.6 = (f32[1,5,8,8,8,128]{5,4,3,2,1,0:T(8,128)S(1)}, f32[1,5,8,8,8,128]{5,4,3,2,1,0:T(8,128)}, u32[]{:S(2)}) copy-start(f32[1,5,8,8,8,128]{5,4,3,2,1,0:T(8,128)} %param.16) | copy-start | bytes 3932164
  48.7 34.1 %collective-permute-start.1 = (f32[2560,128]{1,0:T(8,128)S(1)}, f32[2560,128]{1,0:T(8,128)S(1)}, u32[]{:S(2)}, u32[]{:S(2)}) collective-permute-start(f32[2560,128]{1,0:T(8,128)S(1)} %shard_map.120), channel_id=1, source_target_pairs={{0,16},{1,17},{2,18},{3,19},{4,20},{5,21},{6,22},{7,23},{8,24},{9,... | collective-permute-start | bytes 3932168 | tf_op jit(solution)/shard_map/ppermute | solution.py:28

commit v4 on v3

--- a/solution.py
+++ b/solution.py
@@ -155,15 +155,23 @@
 def volume_of(state, rolled, rate):
     numbers = derivative_numbers()
 
-    def combine(fields, target):
-        result = None
-        for index in range(NP):
-            factor = float(-metric * numbers[target, index])
-            if factor == 0.0:
-                continue
-            term = factor * fields[index]
-            result = term if result is None else result + term
-        return result
+    def derived(fields):
+        even = [fields[index] + fields[NP - 1 - index] for index in range(NP // 2)]
+        odd = [fields[index] - fields[NP - 1 - index] for index in range(NP // 2)]
+        results = [None] * NP
+        for target in range(NP // 2):
+            near = None
+            far = None
+            for index in range(NP // 2):
+                here = float(numbers[target, index])
+                there = float(numbers[target, NP - 1 - index])
+                one = (-0.5 * metric * (here + there)) * even[index]
+                two = (-0.5 * metric * (here - there)) * odd[index]
+                near = one if near is None else near + one
+                far = two if far is None else far + two
+            results[target] = far + near
+            results[NP - 1 - target] = far - near
+        return results
 
     def at(v, i, j):
         return pl.ds(pl.multiple_of(v * NP * NODES + i * NODES + j * NP, NP), NP)
@@ -182,8 +190,8 @@
                     total = total + rolled[shift] * pltpu.roll(part, NP - shift, 0)
                 down[v][i] = total
         for v in range(NV):
-            for i in range(NP):
-                rate[at(v, i, j), :] = combine(across[v], i) + down[v][i]
+            for i, part in enumerate(derived(across[v])):
+                rate[at(v, i, j), :] = part + down[v][i]
         return carry
 
     def along_second(i, carry):
@@ -194,8 +202,8 @@
             for v, part in enumerate(flux(w, velocity, pressure, 1)):
                 across[v][j] = part
         for v in range(NV):
-            for j in range(NP):
-                rate[at(v, i, j), :] = rate[at(v, i, j), :] + combine(across[v], j)
+            for j, part in enumerate(derived(across[v])):
+                rate[at(v, i, j), :] = rate[at(v, i, j), :] + part
         return carry
 
     lax.fori_loop(0, NP, along_first, 0)

time: 84.9 us -> 84.9 us (level)
  no operation moved by 1% of the time
where the time goes in v4:
time: 84.9 us; the launch traced here: 84.6 us
  Pallas kernels  63 us (74%)
  starting transfers between devices  10.1 us (12%)
  other arithmetic  8.36 us (10%)
  local copies, waits for them, and re-layouts  2.37 us (3%)
    pallas_call x5, Pallas kernels, rates_of(): pl.pallas_call(functools.partial(rate_kernel, count), out_shape=[like] *...  63 us
    ppermute x2, starting transfers between devices, shifted(): return lax.ppermute(block, axis, route)  10.1 us
    concatenate x1, other arithmetic, body(): jnp.concatenate([density.reshape(-1, width), momentum.reshape(-1, width),...  2.47 us
    unnamed x28, local copies, waits for them, and re-layouts  2.3 us
    div x1, other arithmetic, body(): return ((state - start) / (TSTEPS * step_size)).reshape(rhs_old.shape)  1.86 us
  transfers between devices with their start and end apart: 2, of which 0 were waited for; matrix products, arithmetic and copies ran while one was open for 5% of the time, Pallas kernels for 61%

profile of v4, /device:TPU:0, one launch (start us, length us, event | category | flops | bytes accessed | tf_op | source)
XLA Modules:
  0.0 84.6 jit_solution(4752811369684956291)
XLA Ops:
  0.0 0.0 copy-start.8
  0.0 0.0 copy-start.11
  0.0 0.0 copy-start.9
  0.0 0.0 copy-start.13
  0.0 0.0 copy-start.12
  0.0 2.5 %pad_maximum_fusion.refs_0_ = f32[2560,128]{1,0:T(8,128)} fusion(f32[512,128]{1,0:T(8,128)} %bitcast.56, f32[1536,128]{1,0:T(8,128)} %bitcast.51, f32[512,128]{1,0:T(8,128)} %bitcast.61), kind=kLoop, calls=%fused_computation.3 | loop fusion | flops 655360 | bytes 2621440 | tf_op jit(solution)/shard_map/concatenate | solution.py:355
  2.5 0.0 copy-start.10
  2.5 0.0 copy-start.1
  2.5 6.0 %collective-permute-start = (f32[2560,128]{1,0:T(8,128)}, f32[2560,128]{1,0:T(8,128)}, u32[]{:S(2)}, u32[]{:S(2)}) collective-permute-start(f32[2560,128]{1,0:T(8,128)} %pad_maximum_fusion.refs_0_), channel_id=1, source_target_pairs={{0,16},{1,17},{2,18},{3,19},{4,20},{5,21},{6,22},{7,23},{8,24},{9,... | collective-permute-start | bytes 3932168 | tf_op jit(solution)/shard_map/ppermute | solution.py:28
  8.5 0.0 copy-done.8
  8.6 0.0 copy-done.11
  8.6 0.0 copy-done.9
  8.6 0.0 copy-done.13
  8.6 0.2 convert_reduce_fusion
  8.8 0.0 copy-done.12
  8.8 0.3 convolution_convert_fusion.refs_5_.refs_6_
  9.1 0.3 convolution_convert_fusion.1.refs_4_.refs_5_
  9.4 0.5 fusion.1.refs_3_.refs_4_
  9.9 0.0 copy-done.10
  9.9 0.1 broadcast_in_dim.2.refs_6_.refs_7_
  10.0 0.0 copy-done.1
  10.0 0.0 copy-start.2
  10.0 0.0 copy-start.4
  10.0 0.0 copy-start.5
  10.0 12.1 %shard_map.118 = f32[2560,128]{1,0:T(8,128)S(1)} custom-call(f32[2560,128]{1,0:T(8,128)} %pad_maximum_fusion.refs_0_, f32[8,768]{1,0:T(8,128)S(1)} %fusion.17.refs_1_.refs_2_, bf16[64,256]{1,0:T(8,128)(2,1)S(1)} %copy-done.1, bf16[768,768]{1,0:T(8,128)(2,1)S(1)} %fusion.1.refs_3_.refs_4_, bf16[128,768]{1,0:T(8,128)(2,1)S(1)} %convolution_convert_fusion.1.refs_4_.refs_5_, ...), custom_call_target="tpu_custom_call" | custom-call | tf_op jit(solution)/shard_map/pallas_call | solution.py:308
  22.2 0.0 copy-done.2
  22.2 0.0 copy-done.4
  22.2 0.0 copy-done.5
  22.2 1.2 %multiply_add_fusion.1.refs_0_ = f32[2560,128]{1,0:T(8,128)} fusion(f32[2560,128]{1,0:T(8,128)S(1)} %shard_map.118, f32[512,128]{1,0:T(8,128)S(1)} %bitcast.57, f32[1536,128]{1,0:T(8,128)S(1)} %bitcast.52, f32[512,128]{1,0:T(8,128)S(1)} %bitcast.62), kind=kLoop, calls=%fused_computation.21 | loop fusion | flops 1310720 | bytes 3932160 | tf_op jit(solution)/shard_map/add | solution.py:421
  23.4 0.0 copy-start
  23.4 1.3 %copy-done = f32[2560,128]{1,0:T(8,128)S(1)} copy-done((f32[2560,128]{1,0:T(8,128)S(1)}, f32[2560,128]{1,0:T(8,128)}, u32[]{:S(2)}) %copy-start) | copy-done | bytes 1310744
  24.8 0.0 copy-start.7
  24.8 10.9 %shard_map.119 = f32[2560,128]{1,0:T(8,128)S(1)} custom-call(f32[2560,128]{1,0:T(8,128)S(1)} %copy-done, f32[8,768]{1,0:T(8,128)S(1)} %fusion.17.refs_1_.refs_2_, bf16[64,256]{1,0:T(8,128)(2,1)S(1)} %copy-done.1, bf16[768,768]{1,0:T(8,128)(2,1)S(1)} %fusion.1.refs_3_.refs_4_, bf16[128,768]{1,0:T(8,128)(2,1)S(1)} %convolution_convert_fusion.1.refs_4_.refs_5_, ...), custom_call_target="tpu_custom_call" | custom-call | tf_op jit(solution)/shard_map/pallas_call | solution.py:308
  35.7 0.0 copy-done.7
  35.7 0.0 copy-start.3
  35.7 0.2 broadcast_multiply_fusion
  35.9 0.9 %copy-done.3 = f32[1,3,8,8,8,128]{5,4,3,2,1,0:T(8,128)S(1)} copy-done((f32[1,3,8,8,8,128]{5,4,3,2,1,0:T(8,128)S(1)}, f32[1,3,8,8,8,128]{5,4,3,2,1,0:T(8,128)}, u32[]{:S(2)}) %copy-start.3) | copy-done | bytes 786456
  36.9 0.3 multiply_add_fusion
  37.2 0.0 collective-permute-done
  37.2 0.2 broadcast_select_fusion.refs_0_
  37.4 0.0 copy-start.6
  37.4 11.3 %shard_map.120 = f32[2560,128]{1,0:T(8,128)S(1)} custom-call(f32[2560,128]{1,0:T(8,128)S(1)} %broadcast_select_fusion.refs_0_, f32[8,768]{1,0:T(8,128)S(1)} %fusion.17.refs_1_.refs_2_, bf16[64,256]{1,0:T(8,128)(2,1)S(1)} %copy-done.1, bf16[768,768]{1,0:T(8,128)(2,1)S(1)} %fusion.1.refs_3_.refs_4_, ...), custom_call_target="tpu_custom_call" | custom-call | tf_op jit(solution)/shard_map/pallas_call | solution.py:308
  48.7 4.0 %collective-permute-start.1 = (f32[2560,128]{1,0:T(8,128)S(1)}, f32[2560,128]{1,0:T(8,128)S(1)}, u32[]{:S(2)}, u32[]{:S(2)}) collective-permute-start(f32[2560,128]{1,0:T(8,128)S(1)} %shard_map.120), channel_id=1, source_target_pairs={{0,16},{1,17},{2,18},{3,19},{4,20},{5,21},{6,22},{7,23},{8,24},{9,... | collective-permute-start | bytes 3932168 | tf_op jit(solution)/shard_map/ppermute | solution.py:28
  52.7 0.0 copy-done.6
  52.7 0.7 multiply_add_fusion.2
  53.4 16.8 %shard_map.121 = (f32[2560,128]{1,0:T(8,128)S(1)}, f32[2560,128]{1,0:T(8,128)S(1)}) custom-call(f32[2560,128]{1,0:T(8,128)S(1)} %get-tuple-element.20.refs_0_, f32[2560,128]{1,0:T(8,128)S(1)} %get-tuple-element.19.refs_1_, f32[8,768]{1,0:T(8,128)S(1)} %fusion.17.refs_1_.refs_2_, bf16[64,256]{1,0:T(8,128)(2,1)S(1)} %copy-done.1, ...), custom_call_target="tpu_custom_call" | custom-call | tf_op jit(solution)/shard_map/pallas_call | solution.py:308
  70.3 0.7 fusion.12.refs_0_
  70.9 11.8 %shard_map.122 = f32[2560,128]{1,0:T(8,128)S(1)} custom-call(f32[2560,128]{1,0:T(8,128)S(1)} %fusion.12.refs_0_, f32[8,768]{1,0:T(8,128)S(1)} %fusion.17.refs_1_.refs_2_, bf16[64,256]{1,0:T(8,128)(2,1)S(1)} %copy-done.1, bf16[768,768]{1,0:T(8,128)(2,1)S(1)} %fusion.1.refs_3_.refs_4_, bf16[128,768]{1,0:T(8,128)(2,1)S(1)} %convolution_convert_fusion.1.refs_4_.refs_5_, ...), custom_call_target="tpu_custom_call" | custom-call | tf_op jit(solution)/shard_map/pallas_call | solution.py:308
  82.7 0.0 collective-permute-done.1
  82.7 1.9 %subtract_multiply_fusion = f32[2560,128]{1,0:T(8,128)} fusion(f32[2560,128]{1,0:T(8,128)S(1)} %collective-permute-done.1, f32[2560,128]{1,0:T(8,128)S(1)} %get-tuple-element.14, f32[2560,128]{1,0:T(8,128)S(1)} %shard_map.120, f32[2560,128]{1,0:T(8,128)S(1)} %fusion.12.refs_0_, f32[2560,128]{1,0:T(8,128)S(1)} %shard_map.122, ...), kind=kLoop, calls=%fused_computation.19 | loop fusion | flops 6553600 | bytes 10485761 | tf_op jit(solution)/shard_map/div | solution.py:443
  (5 shorter events, 0.1 us)
Async XLA Ops:
  0.0 8.5 %copy-start.8 = (s32[1,768]{1,0:T(1,128)S(1)}, s32[1,768]{1,0:T(1,128)}, u32[]{:S(2)}) copy-start(s32[1,768]{1,0:T(1,128)} %param.20) | copy-start | bytes 9220
  0.0 8.6 %copy-start.11 = (s32[1,768]{1,0:T(1,128)S(1)}, s32[1,768]{1,0:T(1,128)}, u32[]{:S(2)}) copy-start(s32[1,768]{1,0:T(1,128)} %param.21) | copy-start | bytes 9220
  0.0 8.6 %copy-start.9 = (s32[1,120]{1,0:T(1,128)S(1)}, s32[1,120]{1,0:T(1,128)}, u32[]{:S(2)}) copy-start(s32[1,120]{1,0:T(1,128)} %param.17) | copy-start | bytes 1444
  0.0 8.6 %copy-start.13 = (s32[1,120]{1,0:T(1,128)S(1)}, s32[1,120]{1,0:T(1,128)}, u32[]{:S(2)}) copy-start(s32[1,120]{1,0:T(1,128)} %param.18) | copy-start | bytes 1444
  0.0 8.8 %copy-start.12 = (s32[1,120]{1,0:T(1,128)S(1)}, s32[1,120]{1,0:T(1,128)}, u32[]{:S(2)}) copy-start(s32[1,120]{1,0:T(1,128)} %param.19) | copy-start | bytes 1444
  2.5 7.4 %copy-start.10 = (f32[8,8]{1,0:T(8,128)S(1)}, f32[8,8]{1,0:T(8,128)}, u32[]{:S(2)}) copy-start(f32[8,8]{1,0:T(8,128)} %constant.26.clone) | copy-start | bytes 772
  2.5 7.5 %copy-start.1 = (bf16[64,256]{1,0:T(8,128)(2,1)S(1)}, bf16[64,256]{1,0:T(8,128)(2,1)}, u32[]{:S(2)}) copy-start(bf16[64,256]{1,0:T(8,128)(2,1)} %constant.25.clone.refs_2_.refs_3_) | copy-start | bytes 98308
  2.5 34.7 %collective-permute-start = (f32[2560,128]{1,0:T(8,128)}, f32[2560,128]{1,0:T(8,128)}, u32[]{:S(2)}, u32[]{:S(2)}) collective-permute-start(f32[2560,128]{1,0:T(8,128)} %pad_maximum_fusion.refs_0_), channel_id=1, source_target_pairs={{0,16},{1,17},{2,18},{3,19},{4,20},{5,21},{6,22},{7,23},{8,24},{9,... | collective-permute-start | bytes 3932168 | tf_op jit(solution)/shard_map/ppermute | solution.py:28
  10.0 12.2 %copy-start.2 = (f32[1,3,8,8,8,128]{5,4,3,2,1,0:T(8,128)S(1)}, f32[1,3,8,8,8,128]{5,4,3,2,1,0:T(8,128)}, u32[]{:S(2)}) copy-start(f32[1,3,8,8,8,128]{5,4,3,2,1,0:T(8,128)} %param.13) | copy-start | bytes 2359300
  10.0 12.2 %copy-start.4 = (f32[1,8,8,8,128]{4,3,2,1,0:T(8,128)S(1)}, f32[1,8,8,8,128]{4,3,2,1,0:T(8,128)}, u32[]{:S(2)}) copy-start(f32[1,8,8,8,128]{4,3,2,1,0:T(8,128)} %param.14) | copy-start | bytes 786436
  10.0 12.2 %copy-start.5 = (f32[1,8,8,8,128]{4,3,2,1,0:T(8,128)S(1)}, f32[1,8,8,8,128]{4,3,2,1,0:T(8,128)}, u32[]{:S(2)}) copy-start(f32[1,8,8,8,128]{4,3,2,1,0:T(8,128)} %param.12) | copy-start | bytes 786436
  23.4 1.3 %copy-start = (f32[2560,128]{1,0:T(8,128)S(1)}, f32[2560,128]{1,0:T(8,128)}, u32[]{:S(2)}) copy-start(f32[2560,128]{1,0:T(8,128)} %multiply_add_fusion.1.refs_0_) | copy-start | bytes 3932164
  24.8 11.0 %copy-start.7 = (f32[1,5,8,8,8,128]{5,4,3,2,1,0:T(8,128)S(1)}, f32[1,5,8,8,8,128]{5,4,3,2,1,0:T(8,128)}, u32[]{:S(2)}) copy-start(f32[1,5,8,8,8,128]{5,4,3,2,1,0:T(8,128)} %param.15) | copy-start | bytes 3932164
  35.7 1.1 %copy-start.3 = (f32[1,3,8,8,8,128]{5,4,3,2,1,0:T(8,128)S(1)}, f32[1,3,8,8,8,128]{5,4,3,2,1,0:T(8,128)}, u32[]{:S(2)}) copy-start(f32[1,3,8,8,8,128]{5,4,3,2,1,0:T(8,128)} %param.13) | copy-start | bytes 2359300
  37.4 15.3 %copy-start.6 = (f32[1,5,8,8,8,128]{5,4,3,2,1,0:T(8,128)S(1)}, f32[1,5,8,8,8,128]{5,4,3,2,1,0:T(8,128)}, u32[]{:S(2)}) copy-start(f32[1,5,8,8,8,128]{5,4,3,2,1,0:T(8,128)} %param.16) | copy-start | bytes 3932164
  48.7 34.1 %collective-permute-start.1 = (f32[2560,128]{1,0:T(8,128)S(1)}, f32[2560,128]{1,0:T(8,128)S(1)}, u32[]{:S(2)}, u32[]{:S(2)}) collective-permute-start(f32[2560,128]{1,0:T(8,128)S(1)} %shard_map.120), channel_id=1, source_target_pairs={{0,16},{1,17},{2,18},{3,19},{4,20},{5,21},{6,22},{7,23},{8,24},{9,... | collective-permute-start | bytes 3932168 | tf_op jit(solution)/shard_map/ppermute | solution.py:28
